TPU v7x, 256 devices: a whole 4x4x8 slice. The times are simulated.
256 devices in a mesh: ctx: 32 (over z, y), head: 8 (over x, core).
Axes of the slice: x: 4, y: 4, z: 8, core: 2. Of those that a mesh axis runs over, the one named last changes fastest.
Arguments:
- queries: bfloat16 [2048, 2048], P(None, 'head'), may hold values from -16 to 16
- prefix_keys: bfloat16 [32768, 2048], P('ctx', 'head'), may hold values from -6 to 6
- prefix_values: bfloat16 [32768, 2048], P('ctx', 'head'), may hold values from -6 to 6
- out_grad: bfloat16 [2048, 2048], P(None, 'head'), may hold values from -6 to 6
- block_lists: int32 [16, 16, 64], P('head'), may hold values from 0 to 511, as said below
- list_counts: int32 [16, 16], P('head'), may hold values from 32 to 64
Outputs:
- query_grad: bfloat16 [2048, 2048], P('ctx', 'head')
- key_grad: bfloat16 [32768, 2048], P(('ctx', 'head'))
- value_grad: bfloat16 [32768, 2048], P(('ctx', 'head'))
Inputs may be any that keep to these rules, and one draw needn't show every extreme that they name: `block_lists`: within a list all 64 entries are distinct block numbers; entries from list_counts on are ignored. Of the live entries of every list at most 8 lie in the blocks of one context slice (slice c holds blocks c * 16 onward), and exactly 8 in one slice.
All inputs are finite; a program needn't handle non-finite values.
Results may differ from a plain program's by a relative error of at most 0.017.
Values may be sent and summed in bfloat16 or wider, within the bound.
A program may use at most 128 MiB of HBM per device.

v0:
```python
import jax
import jax.numpy as jnp
from jax import lax
from jax.sharding import PartitionSpec as P

HD = 128
TILE = 128
BLOCK = 64


masked_score = -1e30


def joined(value, axis, join):
    pieces = jax.tree.map(lambda part: lax.all_gather(part, axis), value)
    head = jax.tree.map(lambda part: part[0], pieces)
    tail = jax.tree.map(lambda part: part[1:], pieces)
    running, _ = lax.scan(lambda running, piece: (join(running, piece), None), head, tail)
    return running


def pair_combine(former, latter):
    joint = jnp.maximum(former[0], latter[0])
    return (joint, former[1] * jnp.exp(former[0] - joint) + latter[1] * jnp.exp(latter[0] - joint))


def local(queries, prefix_keys, prefix_values, out_grad, block_lists, list_counts):
    heads_here = prefix_keys.shape[1] // HD
    slice_len = prefix_keys.shape[0]
    blocks_here = slice_len // BLOCK
    latents = queries.shape[0]
    score_scale = HD ** (-0.5)
    local_ids = block_lists - lax.axis_index("ctx") * blocks_here
    positions = jnp.arange(block_lists.shape[2], dtype=jnp.int32)
    listed = (
        (positions[None, None, :] < list_counts[:, :, None])
        & (local_ids >= 0)
        & (local_ids < blocks_here)
    )
    block_ids = jnp.arange(blocks_here, dtype=jnp.int32)
    chosen = jnp.any(listed[..., None] & (local_ids[..., None] == block_ids), axis=2)
    kept = []
    maxima = []
    totals = []
    for head_index in range(heads_here):
        first_col = head_index * HD
        query_head = queries[:, first_col : first_col + HD]
        key_head = prefix_keys[:, first_col : first_col + HD]
        value_head = prefix_values[:, first_col : first_col + HD]
        grad_head = out_grad[:, first_col : first_col + HD]
        key_mask = jnp.repeat(jnp.repeat(chosen[head_index], TILE, axis=0), BLOCK, axis=1)
        key_use = key_head
        value_use = value_head
        query_use = query_head
        grad_use = grad_head
        scores = score_scale * jnp.einsum(
            "ld,sd->ls", query_head, key_head, preferred_element_type=jnp.float32
        )
        dprobs = jnp.einsum("ld,sd->ls", grad_head, value_head, preferred_element_type=jnp.float32)
        scores = jnp.where(key_mask, scores, masked_score)
        row_max = jnp.max(scores, axis=-1)
        weights = jnp.where(key_mask, jnp.exp(scores - row_max[..., None]), 0.0)
        maxima.append(row_max)
        totals.append(jnp.sum(weights, axis=-1))
        kept.append((scores, dprobs, key_mask, key_use, value_use, query_use, grad_use))
    row_maxima = jnp.stack(maxima)
    row_totals = jnp.stack(totals)
    prob_list = []
    merged_max, merged_total = joined((row_maxima, row_totals), "ctx", pair_combine)
    log_totals = merged_max + jnp.log(merged_total)
    partial_deltas = []
    for head_index in range(heads_here):
        scores, dprobs, key_mask = (kept[head_index][0], kept[head_index][1], kept[head_index][2])
        log_here = log_totals[head_index][..., None]
        attn_probs = jnp.where(key_mask, jnp.exp(scores - log_here), 0.0)
        prob_list.append(attn_probs)
        partial_deltas.append(jnp.sum(attn_probs * dprobs, axis=-1))
    row_deltas = lax.psum(jnp.stack(partial_deltas), "ctx")
    query_terms = []
    key_terms = []
    value_terms = []
    for head_index in range(heads_here):
        scores, dprobs, key_mask, key_use, value_use, query_use, grad_use = kept[head_index]
        attn_probs = prob_list[head_index]
        delta_here = row_deltas[head_index][..., None]
        dscores = (attn_probs * (dprobs - delta_here)).astype(jnp.bfloat16)
        probs_low = attn_probs.astype(jnp.bfloat16)
        query_terms.append(
            score_scale
            * jnp.einsum("ls,sd->ld", dscores, key_use, preferred_element_type=jnp.float32)
        )
        key_terms.append(
            score_scale
            * jnp.einsum("ls,ld->sd", dscores, query_use, preferred_element_type=jnp.float32)
        )
        value_terms.append(
            jnp.einsum("ls,ld->sd", probs_low, grad_use, preferred_element_type=jnp.float32)
        )
    query_term = jnp.concatenate(query_terms, axis=1)
    key_local = jnp.concatenate(key_terms, axis=1).astype(jnp.bfloat16)
    value_local = jnp.concatenate(value_terms, axis=1).astype(jnp.bfloat16)
    own_rows = latents // lax.axis_size("ctx")
    summed = lax.psum(query_term, "ctx")
    query_grad = lax.dynamic_slice_in_dim(summed, lax.axis_index("ctx") * own_rows, own_rows, 0)
    key_grad, value_grad = (
        lax.all_to_all(key_local, "head", split_axis=0, concat_axis=1, tiled=True),
        lax.all_to_all(value_local, "head", split_axis=0, concat_axis=1, tiled=True),
    )
    return (query_grad.astype(jnp.bfloat16), key_grad, value_grad)


def solution(mesh):
    return jax.shard_map(
        local,
        mesh=mesh,
        in_specs=(
            P(None, "head"),
            P("ctx", "head"),
            P("ctx", "head"),
            P(None, "head"),
            P("head", None, None),
            P("head", None),
        ),
        out_specs=(P("ctx", "head"), P(("ctx", "head"), None), P(("ctx", "head"), None)),
        check_vma=False,
    )
```

profile of v0, /device:TPU:2, one launch (start us, length us, event | category | flops | bytes accessed | tf_op | source)
XLA Modules:
  0.0 488.2 jit_solution(2884194299780184191)
XLA Ops:
  0.7 0.9 fusion.39
  1.6 0.6 fusion.33
  2.2 0.1 copy.16
  2.3 0.1 broadcast_in_dim.33
  2.5 0.1 copy.15
  2.5 0.1 broadcast_in_dim.30
  2.7 2.4 fusion.5
  5.1 1.3 fusion.4
  6.5 52.8 %all-gather.2 = f32[32,2,2048]{2,1,0:T(2,128)S(1)} all-gather(f32[1,2,2048]{2,1,0:T(2,128)S(1)} %maximum_bitcast_fusion), channel_id=2, replica_groups=mesh['ctx'=32,'head'=8] {'ctx'}, dimensions={0}, use_global_device_ids=true | all-gather | bytes 540672 | tf_op jit(solution)/shard_map/all_gather | solution.py:15
  59.4 2.1 fusion.3
  61.4 2.1 fusion.2
  63.5 48.3 %all-gather.3 = f32[32,2,2048]{2,1,0:T(2,128)S(1)} all-gather(f32[1,2,2048]{2,1,0:T(2,128)S(1)} %maximum_bitcast_fusion.1), channel_id=3, replica_groups=mesh['ctx'=32,'head'=8] {'ctx'}, dimensions={0}, use_global_device_ids=true | all-gather | bytes 540672 | tf_op jit(solution)/shard_map/all_gather | solution.py:15
  111.9 1.9 while.12
  111.9 0.1 fusion.47
  112.0 0.1 fusion.47
  112.0 0.1 fusion.47
  112.1 0.1 fusion.47
  112.2 0.1 fusion.47
  112.2 0.1 fusion.47
  112.4 0.1 fusion.47
  112.6 0.1 fusion.47
  112.8 0.1 fusion.47
  112.9 0.1 fusion.47
  113.1 0.1 fusion.47
  113.3 0.1 fusion.47
  113.6 0.1 fusion.47
  113.7 0.1 fusion.47
  113.9 9.2 %multiply_reduce_fusion = (f32[2048]{0:T(1024)S(1)}, f32[2048,1024]{0,1:T(8,128)}, f32[2048,1024]{0,1:T(8,128)}) fusion(f32[2048]{0:T(1024)S(1)} %bitcast.110, f32[2048,1024]{0,1:T(8,128)} %copy-done.1, pred[2048,16]{0,1:T(8,128)(4,1)S(1)} %bitcast.98, bf16[1024,256]{1,0:T(8,128)(2,1)} %param.10, bf16[2048,256]{1,0:T(8,128)(2,1)S(1)} %copy-done.3), kind=kOutput, calls=%fused_computation.15 | convolution fusion | flops 549451776 | bytes 26001408 | tf_op jit(solution)/shard_map/ld,sd->ls/dot_general | solution.py:59
  123.1 9.2 %multiply_reduce_fusion.1 = (f32[2048]{0:T(1024)S(1)}, f32[2048,1024]{0,1:T(8,128)}, f32[2048,1024]{0,1:T(8,128)}) fusion(f32[2048]{0:T(1024)S(1)} %bitcast.107, f32[2048,1024]{0,1:T(8,128)} %copy-done, pred[2048,16]{0,1:T(8,128)(4,1)S(1)} %bitcast.95, bf16[1024,256]{1,0:T(8,128)(2,1)S(1)} %copy-done.6, bf16[2048,256]{1,0:T(8,128)(2,1)S(1)} %copy-done.3), kind=kOutput, calls=%fused_computation.16 | convolution fusion | flops 549451776 | bytes 26001408 | tf_op jit(solution)/shard_map/ld,sd->ls/dot_general | solution.py:59
  132.2 140.5 %psum.14 = f32[2,2048]{1,0:T(2,128)S(1)} all-reduce(f32[2,2048]{1,0:T(2,128)S(1)} %pad_maximum_fusion.3), channel_id=1, replica_groups=mesh['ctx'=32,'head'=8] {'ctx'}, use_global_device_ids=true, to_apply=%region_9.10 | all-reduce | flops 4096 | bytes 32768 | tf_op jit(solution)/shard_map/psum | solution.py:78
  272.8 8.0 %multiply_convert_fusion = bf16[2048,1024]{0,1:T(8,128)(2,1)S(1)} fusion(f32[2048,1024]{0,1:T(8,128)} %get-tuple-element.57, f32[2048,1024]{0,1:T(8,128)} %get-tuple-element.70, f32[2048]{0:T(1024)S(1)} %bitcast.112), kind=kLoop, calls=%fused_computation.13 | loop fusion | flops 6291456 | bytes 20979712 | tf_op jit(solution)/shard_map/convert_element_type | solution.py:86
  280.8 2.7 fusion.17
  283.4 10.0 %multiply_convert_fusion.1 = bf16[2048,1024]{0,1:T(8,128)(2,1)} fusion(f32[2048,1024]{0,1:T(8,128)} %get-tuple-element.55, f32[2048,1024]{0,1:T(8,128)} %get-tuple-element.71, f32[2048]{0:T(1024)S(1)} %bitcast.109), kind=kLoop, calls=%fused_computation.14 | loop fusion | flops 6291456 | bytes 20979712 | tf_op jit(solution)/shard_map/convert_element_type | solution.py:86
  293.4 3.5 fusion.16
  296.9 0.9 pad_maximum_fusion.1
  297.8 4.8 all-to-all-start
  302.6 3.0 convolution_multiply_fusion
  305.6 3.1 convolution_multiply_fusion.1
  308.7 4.8 fusion.13
  313.5 0.1 pad_maximum_fusion
  313.7 1.2 fusion.10
  315.0 0.9 pad_maximum_fusion.2
  315.8 4.8 all-to-all-start.1
  320.7 163.2 %all-reduce.1 = bf16[2048,256]{0,1:T(8,128)(2,1)} all-reduce(f32[2048,256]{0,1:T(8,128)S(1)} %pad_maximum_fusion), channel_id=1, replica_groups=mesh['ctx'=32,'head'=8] {'ctx'}, use_global_device_ids=true, to_apply=%region_10.11 | all-reduce | flops 524288 | bytes 3145728 | tf_op jit(solution)/shard_map/psum | solution.py:103
  483.8 0.9 dynamic-slice_convert_fusion
  484.7 0.7 copy.19
  485.5 1.9 copy.20
  487.3 0.8 copy.21
  (51 shorter events, 1.1 us)
Async XLA Ops:
  0.6 4.5 copy-start.4
  0.6 4.5 copy-start.5
  5.1 56.3 %copy-start.1 = (f32[2048,1024]{0,1:T(8,128)}, f32[2048,1024]{0,1:T(8,128)S(1)}, u32[]{:S(2)}) copy-start(f32[2048,1024]{0,1:T(8,128)S(1)} %get-tuple-element.67) | copy-start | bytes 25165828
  6.5 57.0 %copy-start = (f32[2048,1024]{0,1:T(8,128)}, f32[2048,1024]{0,1:T(8,128)S(1)}, u32[]{:S(2)}) copy-start(f32[2048,1024]{0,1:T(8,128)S(1)} %get-tuple-element.69) | copy-start | bytes 25165828
  59.3 54.5 %copy-start.3 = (bf16[2048,256]{1,0:T(8,128)(2,1)S(1)}, bf16[2048,256]{1,0:T(8,128)(2,1)}, u32[]{:S(2)}) copy-start(bf16[2048,256]{1,0:T(8,128)(2,1)} %param.11) | copy-start | bytes 3145732
  113.8 9.2 %copy-start.6 = (bf16[1024,256]{1,0:T(8,128)(2,1)S(1)}, bf16[1024,256]{1,0:T(8,128)(2,1)}, u32[]{:S(2)}) copy-start(bf16[1024,256]{1,0:T(8,128)(2,1)} %param.10) | copy-start | bytes 1572868
  280.8 12.6 %copy-start.2 = (bf16[2048,1024]{0,1:T(8,128)(2,1)}, bf16[2048,1024]{0,1:T(8,128)(2,1)S(1)}, u32[]{:S(2)}) copy-start(bf16[2048,1024]{0,1:T(8,128)(2,1)S(1)} %multiply_convert_fusion) | copy-start | bytes 12582916
  297.8 18.0 %all-to-all-start = ((bf16[8,128,256]{2,1,0:T(8,128)(2,1)}), bf16[8,128,256]{2,1,0:T(8,128)(2,1)}, u32[]{:S(2)}, u32[]{:S(2)}) async-start(bf16[8,128,256]{2,1,0:T(8,128)(2,1)} %pad_maximum_fusion.1), calls=%async_computation | async-start | bytes 1048576 | tf_op jit(solution)/shard_map/all_to_all | solution.py:106
  305.6 8.1 %slice-start = ((s8[8388608]{0:T(1024)(128)(4,1)}), s8[4194304]{0:T(1024)(128)(4,1)S(1)}, s32[]{:S(2)}) async-start(s8[8388608]{0:T(1024)(128)(4,1)} %bitcast.88), calls=%async_computation.2 | async-start | bytes 8388608
  308.7 5.0 %slice-start.1 = ((s8[8388608]{0:T(1024)(128)(4,1)}), s8[4194304]{0:T(1024)(128)(4,1)S(1)}, s32[]{:S(2)}) async-start(s8[8388608]{0:T(1024)(128)(4,1)} %bitcast.88), calls=%async_computation.3 | async-start | bytes 8388608
  315.8 171.5 %all-to-all-start.1 = ((bf16[8,128,256]{2,1,0:T(8,128)(2,1)}), bf16[8,128,256]{2,1,0:T(8,128)(2,1)S(1)}, u32[]{:S(2)}, u32[]{:S(2)}) async-start(bf16[8,128,256]{2,1,0:T(8,128)(2,1)} %pad_maximum_fusion.2), calls=%async_computation.1 | async-start | bytes 1048576 | tf_op jit(solution)/shard_map/all_to_all | solution.py:107
where the time goes:
time: 489 us; the launch traced here: 488 us
  blocking collectives  405 us (83%)
  matrix products  40.4 us (8%)
  other arithmetic  27.1 us (6%)
  starting transfers between devices  9.64 us (2%)
  local copies, waits for them, and re-layouts  4.93 us (1%)
    psum x1, blocking collectives, local(): summed = lax.psum(query_term, 'ctx')  163 us
    psum x1, blocking collectives, local(): row_deltas = lax.psum(jnp.stack(partial_deltas), 'ctx')  141 us
    all_gather x2, blocking collectives, joined(): pieces = jax.tree.map(lambda part: lax.all_gather(part, axis), value)  101 us
    dot_general x2, matrix products, local(): jnp.einsum('ld,sd->ls', grad_head, value_head, preferred_element_type=jnp...  18.4 us
    convert_element_type x2, other arithmetic, local(): dscores = (attn_probs * (dprobs - delta_here)).astype(jnp.bfloat16)  17.9 us
  transfers between devices with their start and end apart: 2, of which 0 were waited for; matrix products, arithmetic and copies ran while one was open for 3% of the time, Pallas kernels for 0%

commit v1 on v0

v1 whole, which is shorter than its diff:
```python
import functools

import jax
import jax.numpy as jnp
from jax import lax
from jax.experimental import pallas as pl
from jax.experimental.pallas import tpu as pltpu
from jax.sharding import PartitionSpec as P

HD = 128
TILE = 128
BLOCK = 64
MOST = 8
NEAR = 2
Y = 4
MASKED = -1e30
SCALE = HD ** -0.5
SCALE2 = SCALE * 1.4426950408889634
MESH = pl.DeviceIdType.MESH
F32 = jnp.float32
BF16 = jnp.bfloat16
VMEM_LIMIT = 48 * 1024 * 1024


def dot_nt(a, b):
    return lax.dot_general(a, b, (((1,), (1,)), ((), ())), preferred_element_type=F32)


def dot_nn(a, b):
    return lax.dot_general(a, b, (((1,), (0,)), ((), ())), preferred_element_type=F32)


def dot_tn(a, b):
    return lax.dot_general(a, b, (((0,), (0,)), ((), ())), preferred_element_type=F32)


def picked(ref, table, row, head, first, slots):
    cols = pl.ds(head * HD, HD)
    parts = []
    for slot in range(first, first + slots):
        start = pl.multiple_of(table[row, slot] * BLOCK, BLOCK)
        parts.append(ref[pl.ds(start, BLOCK), cols])
    return jnp.concatenate(parts, axis=0)


def slot_table(lists, counts_row, me, blocks_here):
    tiles, sel = lists.shape
    eye = lax.broadcasted_iota(jnp.int32, (tiles, tiles), 0) == lax.broadcasted_iota(jnp.int32, (tiles, tiles), 1)
    counts = jnp.sum(jnp.where(eye, counts_row, 0), axis=1, keepdims=True)
    local = lists - me * blocks_here
    pos = lax.broadcasted_iota(jnp.int32, (tiles, sel), 1)
    listed = (pos < counts) & (local >= 0) & (local < blocks_here)
    flags = jnp.where(listed, 1.0, 0.0)
    before = lax.broadcasted_iota(jnp.int32, (sel, sel), 0) < lax.broadcasted_iota(jnp.int32, (sel, sel), 1)
    rank = dot_nn(flags.astype(BF16), jnp.where(before, 1.0, 0.0).astype(BF16))
    ids = local.astype(F32)
    lane = lax.broadcasted_iota(jnp.int32, (tiles, 128), 1)
    total = jnp.sum(flags, axis=1, keepdims=True)
    table = jnp.where(lane == MOST, total, 0.0)
    for slot in range(MOST):
        value = jnp.sum(jnp.where(listed & (rank == float(slot)), ids, 0.0), axis=1, keepdims=True)
        table = jnp.where(lane == slot, value, table)
    return table.astype(jnp.int32)


def stats_kernel(heads, tiles, unroll, lists_ref, counts_ref, q_ref, k_ref, v_ref, g_ref, stats_ref, table_out, table_vmem, table, sem):
    me = lax.axis_index("ctx")
    blocks_here = k_ref.shape[0] // BLOCK
    for head in range(heads):
        table_vmem[pl.ds(head * tiles, tiles), :] = slot_table(
            lists_ref[head], counts_ref[pl.ds(head, 1), :], me, blocks_here
        )
    copy = pltpu.make_async_copy(table_vmem, table, sem)
    copy.start()
    table_out[...] = table_vmem[...]
    copy.wait()

    def part(head, tile, first, slots):
        row = head * tiles + tile
        live = (table[row, MOST] - first) * BLOCK
        rows = pl.ds(pl.multiple_of(tile * TILE, TILE), TILE)
        cols = pl.ds(head * HD, HD)
        keys = picked(k_ref, table, row, head, first, slots)
        vals = picked(v_ref, table, row, head, first, slots)
        scores = dot_nt(keys, q_ref[rows, cols]) * SCALE2
        dprobs = dot_nt(vals, g_ref[rows, cols])
        mask = lax.broadcasted_iota(jnp.int32, scores.shape, 0) < live
        scores = jnp.where(mask, scores, MASKED)
        top = jnp.max(scores, axis=0, keepdims=True)
        weights = jnp.where(mask, jnp.exp2(scores - top), 0.0)
        total = jnp.sum(weights, axis=0, keepdims=True)
        delta = jnp.sum(weights * dprobs, axis=0, keepdims=True)
        return top, total, delta

    def near(step, carry):
        for inner in range(unroll):
            for head in range(heads):
                tile = step * unroll + inner
                row = head * tiles + tile
                top, total, delta = part(head, tile, 0, NEAR)
                stats_ref[row, pl.ds(0, 1), :] = top
                stats_ref[row, pl.ds(1, 1), :] = total
                stats_ref[row, pl.ds(2, 1), :] = delta
        return carry

    lax.fori_loop(0, tiles // unroll, near, 0)

    def far(tile, carry):
        for head in range(heads):
            row = head * tiles + tile

            @pl.when(table[row, MOST] > NEAR)
            def _():
                top, total, delta = part(head, tile, NEAR, MOST - NEAR)
                old = stats_ref[row, pl.ds(0, 1), :]
                joint = jnp.maximum(old, top)
                a = jnp.exp2(old - joint)
                b = jnp.exp2(top - joint)
                stats_ref[row, pl.ds(0, 1), :] = joint
                stats_ref[row, pl.ds(1, 1), :] = a * stats_ref[row, pl.ds(1, 1), :] + b * total
                stats_ref[row, pl.ds(2, 1), :] = a * stats_ref[row, pl.ds(2, 1), :] + b * delta

        return carry

    lax.fori_loop(0, tiles, far, 0)


def join_kernel(n, stats_ref, out_ref, recv, merged, send1, recv1, send2, recv2):
    me = lax.axis_index("ctx")
    head = lax.axis_index("head")
    barrier = pltpu.get_barrier_semaphore()

    def greet(step, carry):
        peer = lax.rem(me + step, n)
        pl.semaphore_signal(barrier, inc=1, device_id=(peer, head), device_id_type=MESH)
        return carry

    lax.fori_loop(1, n, greet, 0)
    pl.semaphore_wait(barrier, n - 1)

    def first(peer, source):
        return pltpu.make_async_remote_copy(
            src_ref=stats_ref.at[peer], dst_ref=recv.at[source], send_sem=send1.at[peer], recv_sem=recv1.at[source],
            device_id=(peer, head), device_id_type=MESH,
        )

    def second(peer, source):
        return pltpu.make_async_remote_copy(
            src_ref=merged.at[source], dst_ref=merged.at[source], send_sem=send2.at[peer], recv_sem=recv2.at[source],
            device_id=(peer, head), device_id_type=MESH,
        )

    def over(body):
        def step(i, carry):
            body(lax.rem(me + i, n))
            return carry

        lax.fori_loop(1, n, step, 0)

    over(lambda peer: first(peer, me).start())
    recv[me] = stats_ref[me]
    over(lambda peer: first(peer, peer).wait_recv())
    pieces = recv[...]
    tops = pieces[:, 0, :]
    top = jnp.max(tops, axis=0, keepdims=True)
    share = jnp.exp2(tops - top)
    total = jnp.sum(share * pieces[:, 1, :], axis=0, keepdims=True)
    delta = jnp.sum(share * pieces[:, 2, :], axis=0, keepdims=True)
    merged[me, pl.ds(0, 1), :] = top + jnp.log2(total)
    merged[me, pl.ds(1, 1), :] = delta / total
    over(lambda peer: second(peer, me).start())
    over(lambda peer: first(peer, me).wait_send())
    over(lambda peer: second(peer, peer).wait_recv())
    out_ref[...] = merged[...]
    over(lambda peer: second(peer, me).wait_send())


def grads_kernel(heads, tiles, unroll, table, stats_ref, q_ref, k_ref, v_ref, g_ref, dq_ref, dk_ref, dv_ref, dk_acc, dv_acc):
    dk_acc[...] = jnp.zeros_like(dk_acc)
    dv_acc[...] = jnp.zeros_like(dv_acc)

    def part(head, tile, first, slots):
        row = head * tiles + tile
        live = (table[row, MOST] - first) * BLOCK
        rows = pl.ds(pl.multiple_of(tile * TILE, TILE), TILE)
        cols = pl.ds(head * HD, HD)
        keys = picked(k_ref, table, row, head, first, slots)
        vals = picked(v_ref, table, row, head, first, slots)
        query = q_ref[rows, cols]
        grad = g_ref[rows, cols]
        scores = dot_nt(keys, query) * SCALE2
        dprobs = dot_nt(vals, grad)
        mask = lax.broadcasted_iota(jnp.int32, scores.shape, 0) < live
        log_total = stats_ref[row, pl.ds(0, 1), :]
        delta = stats_ref[row, pl.ds(1, 1), :]
        probs = jnp.where(mask, jnp.exp2(scores - log_total), 0.0)
        dscores = (probs * (dprobs - delta)).astype(BF16)
        low = probs.astype(BF16)
        dkeys = dot_nn(dscores, query)
        dvals = dot_nn(low, grad)
        dquery = dot_tn(dscores, keys) * SCALE
        for slot in range(slots):
            start = pl.multiple_of(table[row, first + slot] * BLOCK, BLOCK)
            dk_acc[head, pl.ds(start, BLOCK), :] += dkeys[slot * BLOCK : (slot + 1) * BLOCK]
            dv_acc[head, pl.ds(start, BLOCK), :] += dvals[slot * BLOCK : (slot + 1) * BLOCK]
        return dquery

    def near(step, carry):
        for inner in range(unroll):
            for head in range(heads):
                tile = step * unroll + inner
                rows = pl.ds(pl.multiple_of(tile * TILE, TILE), TILE)
                dq_ref[rows, pl.ds(head * HD, HD)] = part(head, tile, 0, NEAR).astype(BF16)
        return carry

    lax.fori_loop(0, tiles // unroll, near, 0)

    def far(tile, carry):
        for head in range(heads):
            row = head * tiles + tile

            @pl.when(table[row, MOST] > NEAR)
            def _():
                rows = pl.ds(pl.multiple_of(tile * TILE, TILE), TILE)
                cols = pl.ds(head * HD, HD)
                extra = part(head, tile, NEAR, MOST - NEAR)
                dq_ref[rows, cols] = (dq_ref[rows, cols].astype(F32) + extra).astype(BF16)

        return carry

    lax.fori_loop(0, tiles, far, 0)
    for head in range(heads):
        cols = pl.ds(head * HD, HD)
        dk_ref[:, cols] = (dk_acc[head] * SCALE).astype(BF16)
        dv_ref[:, cols] = dv_acc[head].astype(BF16)


def swap_kernel(n_ctx, n_head, dq_ref, dk_ref, dv_ref, oq_ref, ok_ref, ov_ref,
                ybuf, zsend, zbuf, ssend, srecv, ysend, yrecv, zsend_sem, zrecv, own):
    me = lax.axis_index("ctx")
    head = lax.axis_index("head")
    n_z = n_ctx // Y
    z = me // Y
    y = lax.rem(me, Y)
    tokens = ok_ref.shape[0]
    width = dk_ref.shape[1]
    barrier = pltpu.get_barrier_semaphore()

    def at_head(i):
        return (me, lax.rem(head + i, n_head))

    def at_y(i):
        return (z * Y + lax.rem(y + i, Y), head)

    def at_z(i):
        return (lax.rem(z + i, n_z) * Y + y, head)

    for count, where in ((n_head, at_head), (Y, at_y), (n_z, at_z)):
        for i in range(1, count):
            pl.semaphore_signal(barrier, inc=1, device_id=where(i), device_id_type=MESH)
    pl.semaphore_wait(barrier, n_head + Y + n_z - 3)

    def token_copy(which, i, source):
        src, dst = ((dk_ref, ok_ref), (dv_ref, ov_ref))[which]
        peer = lax.rem(head + i, n_head)
        return pltpu.make_async_remote_copy(
            src_ref=src.at[pl.ds(pl.multiple_of(peer * tokens, tokens), tokens), :],
            dst_ref=dst.at[:, pl.ds(pl.multiple_of(source * width, width), width)],
            send_sem=ssend.at[which, i], recv_sem=srecv.at[which, source],
            device_id=(me, peer), device_id_type=MESH,
        )

    def y_copy(zz, i, source):
        peer = lax.rem(y + i, Y)
        return pltpu.make_async_remote_copy(
            src_ref=dq_ref.at[zz, peer], dst_ref=ybuf.at[zz, source],
            send_sem=ysend.at[zz, i], recv_sem=yrecv.at[zz, source],
            device_id=(z * Y + peer, head), device_id_type=MESH,
        )

    def z_copy(i, source):
        peer = lax.rem(z + i, n_z)
        return pltpu.make_async_remote_copy(
            src_ref=zsend.at[peer], dst_ref=zbuf.at[source],
            send_sem=zsend_sem.at[i], recv_sem=zrecv.at[source],
            device_id=(peer * Y + y, head), device_id_type=MESH,
        )

    for i in range(1, n_z + 1):
        zz = lax.rem(z + i, n_z)
        for j in (2, 1, 3):
            y_copy(zz, j, y).start()
    for i in range(1, n_head):
        for which in range(2):
            token_copy(which, i, head).start()
    mine = []
    for which in range(2):
        src, dst = ((dk_ref, ok_ref), (dv_ref, ov_ref))[which]
        copy = pltpu.make_async_copy(
            src.at[pl.ds(pl.multiple_of(head * tokens, tokens), tokens), :],
            dst.at[:, pl.ds(pl.multiple_of(head * width, width), width)],
            own.at[which],
        )
        copy.start()
        mine.append(copy)

    for i in range(1, n_z + 1):
        zz = lax.rem(z + i, n_z)
        total = dq_ref[zz, y].astype(F32)
        for j in range(1, Y):
            source = lax.rem(y + j, Y)
            y_copy(zz, j, source).wait_recv()
            total = total + ybuf[zz, source].astype(F32)
        if i < n_z:
            zsend[zz] = total.astype(BF16)
            z_copy(i, z).start()
    for i in range(1, n_z):
        source = lax.rem(z + i, n_z)
        z_copy(i, source).wait_recv()
        total = total + zbuf[source].astype(F32)
    oq_ref[...] = total.astype(BF16)
    for copy in mine:
        copy.wait()
    for i in range(1, n_head):
        for which in range(2):
            token_copy(which, i, lax.rem(head + i, n_head)).wait_recv()
    for i in range(1, n_z + 1):
        zz = lax.rem(z + i, n_z)
        for j in range(1, Y):
            y_copy(zz, j, y).wait_send()
    for i in range(1, n_z):
        z_copy(i, z).wait_send()
    for i in range(1, n_head):
        for which in range(2):
            token_copy(which, i, head).wait_send()


def local(n_ctx, n_head, queries, prefix_keys, prefix_values, out_grad, block_lists, list_counts):
    latents, width = queries.shape
    tokens = prefix_keys.shape[0]
    heads = width // HD
    tiles = latents // TILE
    rows = heads * tiles
    n_z = n_ctx // Y
    own = latents // n_ctx
    vmem = pl.BlockSpec(memory_space=pltpu.VMEM)
    smem = pl.BlockSpec(memory_space=pltpu.SMEM)
    anyplace = pl.BlockSpec(memory_space=pl.ANY)
    stats, table = pl.pallas_call(
        functools.partial(stats_kernel, heads, tiles, 4),
        name="local_stats",
        out_shape=(jax.ShapeDtypeStruct((rows, 3, TILE), F32), jax.ShapeDtypeStruct((rows, 128), jnp.int32)),
        in_specs=[vmem] * 6,
        out_specs=(vmem, vmem),
        scratch_shapes=[pltpu.VMEM((rows, 128), jnp.int32), pltpu.SMEM((rows, 128), jnp.int32), pltpu.SemaphoreType.DMA],
        compiler_params=pltpu.CompilerParams(vmem_limit_bytes=VMEM_LIMIT),
    )(block_lists, list_counts, queries, prefix_keys, prefix_values, out_grad)
    totals = pl.pallas_call(
        functools.partial(join_kernel, n_ctx),
        name="join_stats",
        out_shape=jax.ShapeDtypeStruct((rows, 2, TILE), F32),
        in_specs=[vmem],
        out_specs=vmem,
        scratch_shapes=[
            pltpu.VMEM((n_ctx, 3, TILE), F32),
            pltpu.VMEM((n_ctx, 2, TILE), F32),
            pltpu.SemaphoreType.DMA((n_ctx,)),
            pltpu.SemaphoreType.DMA((n_ctx,)),
            pltpu.SemaphoreType.DMA((n_ctx,)),
            pltpu.SemaphoreType.DMA((n_ctx,)),
        ],
        compiler_params=pltpu.CompilerParams(collective_id=0, has_side_effects=True),
    )(stats)
    dq, dk, dv = pl.pallas_call(
        functools.partial(grads_kernel, heads, tiles, 4),
        name="local_grads",
        out_shape=(
            jax.ShapeDtypeStruct((latents, width), BF16),
            jax.ShapeDtypeStruct((tokens, width), BF16),
            jax.ShapeDtypeStruct((tokens, width), BF16),
        ),
        in_specs=[smem] + [vmem] * 5,
        out_specs=(vmem, vmem, vmem),
        scratch_shapes=[pltpu.VMEM((heads, tokens, HD), F32), pltpu.VMEM((heads, tokens, HD), F32)],
        compiler_params=pltpu.CompilerParams(vmem_limit_bytes=VMEM_LIMIT),
    )(table, totals, queries, prefix_keys, prefix_values, out_grad)
    piece = tokens // n_head
    return pl.pallas_call(
        functools.partial(swap_kernel, n_ctx, n_head),
        name="swap_grads",
        out_shape=(
            jax.ShapeDtypeStruct((own, width), BF16),
            jax.ShapeDtypeStruct((piece, n_head * width), BF16),
            jax.ShapeDtypeStruct((piece, n_head * width), BF16),
        ),
        in_specs=[vmem, vmem, vmem],
        out_specs=(vmem, vmem, vmem),
        scratch_shapes=[
            pltpu.VMEM((n_z, Y, own, width), BF16),
            pltpu.VMEM((n_z, own, width), BF16),
            pltpu.VMEM((n_z, own, width), BF16),
            pltpu.SemaphoreType.DMA((2, n_head)),
            pltpu.SemaphoreType.DMA((2, n_head)),
            pltpu.SemaphoreType.DMA((n_z, Y)),
            pltpu.SemaphoreType.DMA((n_z, Y)),
            pltpu.SemaphoreType.DMA((n_z,)),
            pltpu.SemaphoreType.DMA((n_z,)),
            pltpu.SemaphoreType.DMA((2,)),
        ],
        compiler_params=pltpu.CompilerParams(collective_id=1, has_side_effects=True, vmem_limit_bytes=VMEM_LIMIT),
    )(dq.reshape(n_z, Y, own, width), dk, dv)


def solution(mesh):
    return jax.shard_map(
        functools.partial(local, mesh.shape["ctx"], mesh.shape["head"]),
        mesh=mesh,
        in_specs=(
            P(None, "head"),
            P("ctx", "head"),
            P("ctx", "head"),
            P(None, "head"),
            P("head", None, None),
            P("head", None),
        ),
        out_specs=(P("ctx", "head"), P(("ctx", "head"), None), P(("ctx", "head"), None)),
        check_vma=False,
    )
```

time: 489 us -> 69.5 us (0.14)
  the two profiles are of different devices: /device:TPU:2 before, /device:TPU:1 now
where the time goes in v1:
time: 69.5 us; the launch traced here: 69.1 us
  Pallas kernels  58.8 us (85%)
  local copies, waits for them, and re-layouts  9.51 us (14%)
  between operations  0.73 us (1%)
    pallas_call x1, Pallas kernels, local(): pl.pallas_call(functools.partial(join_kernel, n_ctx), name='join_stats',...  23 us
    pallas_call x1, Pallas kernels, local(): pl.pallas_call(functools.partial(swap_kernel, n_ctx, n_head), name='swap_...  21.8 us
    pallas_call x1, Pallas kernels, local(): pl.pallas_call(functools.partial(grads_kernel, heads, tiles, 4), name='lo...  9.74 us
    unnamed x27, local copies, waits for them, and re-layouts  9.51 us
    pallas_call x1, Pallas kernels, local(): pl.pallas_call(functools.partial(stats_kernel, heads, tiles, 4), name='lo...  4.24 us

profile of v1, /device:TPU:1, one launch (start us, length us, event | category | flops | bytes accessed | tf_op | source)
XLA Modules:
  0.0 69.1 jit_solution(17136974174755275702)
XLA Ops:
  0.6 0.0 copy-start
  0.6 1.2 %copy-done = bf16[2048,256]{1,0:T(8,128)(2,1)S(1)} copy-done((bf16[2048,256]{1,0:T(8,128)(2,1)S(1)}, bf16[2048,256]{1,0:T(8,128)(2,1)}, u32[]{:S(2)}) %copy-start) | copy-done | bytes 1048600
  1.9 0.0 copy-start.2
  1.9 1.2 %copy-done.2 = bf16[2048,256]{1,0:T(8,128)(2,1)S(1)} copy-done((bf16[2048,256]{1,0:T(8,128)(2,1)S(1)}, bf16[2048,256]{1,0:T(8,128)(2,1)}, u32[]{:S(2)}) %copy-start.2) | copy-done | bytes 1048600
  3.1 0.0 copy-start.4
  3.1 1.0 %copy-done.4 = bf16[1024,256]{1,0:T(8,128)(2,1)S(1)} copy-done((bf16[1024,256]{1,0:T(8,128)(2,1)S(1)}, bf16[1024,256]{1,0:T(8,128)(2,1)}, u32[]{:S(2)}) %copy-start.4) | copy-done | bytes 524312
  4.1 0.0 copy-start.6
  4.1 1.0 %copy-done.6 = bf16[1024,256]{1,0:T(8,128)(2,1)S(1)} copy-done((bf16[1024,256]{1,0:T(8,128)(2,1)S(1)}, bf16[1024,256]{1,0:T(8,128)(2,1)}, u32[]{:S(2)}) %copy-start.6) | copy-done | bytes 524312
  5.2 0.0 copy-start.10
  5.2 0.7 %copy-done.10 = s32[2,16,64]{2,1,0:T(8,128)S(1)} copy-done((s32[2,16,64]{2,1,0:T(8,128)S(1)}, s32[2,16,64]{2,1,0:T(8,128)}, u32[]{:S(2)}) %copy-start.10) | copy-done | bytes 8216
  5.9 0.0 copy-start.11
  5.9 0.7 copy-done.11
  6.6 0.0 copy-start.1
  6.6 0.0 copy-start.3
  6.6 0.0 copy-start.5
  6.6 0.0 copy-start.7
  6.6 4.2 %local_stats.1 = (f32[32,3,128]{2,1,0:T(4,128)S(1)}, s32[32,128]{1,0:T(8,128)S(1)}) custom-call(s32[2,16,64]{2,1,0:T(8,128)S(1)} %copy-done.10, s32[2,16]{1,0:T(2,128)S(1)} %copy-done.11, bf16[2048,256]{1,0:T(8,128)(2,1)S(1)} %copy-done, bf16[1024,256]{1,0:T(8,128)(2,1)S(1)} %copy-done.4, bf16[1024,256]{1,0:T(8,128)(2,1)S(1)} %copy-done.6, ...), custom_call_target="tpu_custom_call" | custom-call | tf_op jit(solution)/shard_map/local_stats/pallas_call | solution.py:349
  10.8 0.0 copy-start.9
  10.8 0.6 copy-done.9
  11.5 23.0 %join_stats.1.stats_ref = f32[32,2,128]{2,1,0:T(2,128)} custom-call(f32[32,3,128]{2,1,0:T(4,128)} %copy-done.9), custom_call_target="tpu_custom_call" | custom-call | tf_op jit(solution)/shard_map/join_stats/pallas_call | solution.py:358
  34.5 0.0 copy-done.1
  34.5 0.0 copy-done.3
  34.5 0.0 copy-done.5
  34.5 0.0 copy-done.7
  34.5 0.0 copy-start.8
  34.6 0.7 %copy-done.8 = f32[32,2,128]{2,1,0:T(2,128)S(1)} copy-done((f32[32,2,128]{2,1,0:T(2,128)S(1)}, f32[32,2,128]{2,1,0:T(2,128)}, u32[]{:S(2)}) %copy-start.8) | copy-done | bytes 32792
  35.3 9.7 %local_grads.1 = (bf16[2048,256]{1,0:T(8,128)(2,1)S(1)}, bf16[1024,256]{1,0:T(8,128)(2,1)S(1)}, bf16[1024,256]{1,0:T(8,128)(2,1)S(1)}) custom-call(s32[32,128]{1,0:T(8,128)S(1)} %get-tuple-element.8.table, f32[32,2,128]{2,1,0:T(2,128)S(1)} %copy-done.8, bf16[2048,256]{1,0:T(8,128)(2,1)S(1)} %copy-done.1, bf16[1024,256]{1,0:T(8,128)(2,1)S(1)} %copy-done.5, ...), custom_call_target="tpu_custom_call" | custom-call | tf_op jit(solution)/shard_map/local_grads/pallas_call | solution.py:374
  45.1 21.8 %swap_grads.1 = (bf16[64,256]{1,0:T(8,128)(2,1)S(1)}, bf16[128,2048]{1,0:T(8,128)(2,1)S(1)}, bf16[128,2048]{1,0:T(8,128)(2,1)S(1)}) custom-call(bf16[8,4,64,256]{3,2,1,0:T(8,128)(2,1)S(1)} %bitcast.1, bf16[1024,256]{1,0:T(8,128)(2,1)S(1)} %get-tuple-element.11.dk_ref, bf16[1024,256]{1,0:T(8,128)(2,1)S(1)} %get-tuple-element.12.dv_ref), custom_call_target="tpu_custom_call" | custom-call | tf_op jit(solution)/shard_map/swap_grads/pallas_call | solution.py:388
  66.9 0.6 copy.12
  67.5 0.8 %copy.13 = bf16[128,2048]{1,0:T(8,128)(2,1)} copy(bf16[128,2048]{1,0:T(8,128)(2,1)S(1)} %get-tuple-element.17) | data formatting | bytes 1048576
  68.3 0.8 %copy.14 = bf16[128,2048]{1,0:T(8,128)(2,1)} copy(bf16[128,2048]{1,0:T(8,128)(2,1)S(1)} %get-tuple-element.18) | data formatting | bytes 1048576
Async XLA Ops:
  0.6 1.2 %copy-start = (bf16[2048,256]{1,0:T(8,128)(2,1)S(1)}, bf16[2048,256]{1,0:T(8,128)(2,1)}, u32[]{:S(2)}) copy-start(bf16[2048,256]{1,0:T(8,128)(2,1)} %q_ref.3) | copy-start | bytes 3145732
  1.9 1.2 %copy-start.2 = (bf16[2048,256]{1,0:T(8,128)(2,1)S(1)}, bf16[2048,256]{1,0:T(8,128)(2,1)}, u32[]{:S(2)}) copy-start(bf16[2048,256]{1,0:T(8,128)(2,1)} %g_ref.3) | copy-start | bytes 3145732
  3.1 1.0 %copy-start.4 = (bf16[1024,256]{1,0:T(8,128)(2,1)S(1)}, bf16[1024,256]{1,0:T(8,128)(2,1)}, u32[]{:S(2)}) copy-start(bf16[1024,256]{1,0:T(8,128)(2,1)} %k_ref.3) | copy-start | bytes 1572868
  4.1 1.0 %copy-start.6 = (bf16[1024,256]{1,0:T(8,128)(2,1)S(1)}, bf16[1024,256]{1,0:T(8,128)(2,1)}, u32[]{:S(2)}) copy-start(bf16[1024,256]{1,0:T(8,128)(2,1)} %v_ref.3) | copy-start | bytes 1572868
  5.2 0.7 %copy-start.10 = (s32[2,16,64]{2,1,0:T(8,128)S(1)}, s32[2,16,64]{2,1,0:T(8,128)}, u32[]{:S(2)}) copy-start(s32[2,16,64]{2,1,0:T(8,128)} %lists_ref.1) | copy-start | bytes 24580
  5.9 0.7 copy-start.11
  6.6 27.9 %copy-start.1 = (bf16[2048,256]{1,0:T(8,128)(2,1)S(1)}, bf16[2048,256]{1,0:T(8,128)(2,1)}, u32[]{:S(2)}) copy-start(bf16[2048,256]{1,0:T(8,128)(2,1)} %q_ref.3) | copy-start | bytes 3145732
  6.6 28.0 %copy-start.3 = (bf16[2048,256]{1,0:T(8,128)(2,1)S(1)}, bf16[2048,256]{1,0:T(8,128)(2,1)}, u32[]{:S(2)}) copy-start(bf16[2048,256]{1,0:T(8,128)(2,1)} %g_ref.3) | copy-start | bytes 3145732
  6.6 28.0 %copy-start.5 = (bf16[1024,256]{1,0:T(8,128)(2,1)S(1)}, bf16[1024,256]{1,0:T(8,128)(2,1)}, u32[]{:S(2)}) copy-start(bf16[1024,256]{1,0:T(8,128)(2,1)} %k_ref.3) | copy-start | bytes 1572868
  6.6 28.0 %copy-start.7 = (bf16[1024,256]{1,0:T(8,128)(2,1)S(1)}, bf16[1024,256]{1,0:T(8,128)(2,1)}, u32[]{:S(2)}) copy-start(bf16[1024,256]{1,0:T(8,128)(2,1)} %v_ref.3) | copy-start | bytes 1572868
  10.8 0.6 copy-start.9
  34.5 0.8 %copy-start.8 = (f32[32,2,128]{2,1,0:T(2,128)S(1)}, f32[32,2,128]{2,1,0:T(2,128)}, u32[]{:S(2)}) copy-start(f32[32,2,128]{2,1,0:T(2,128)} %join_stats.1.stats_ref) | copy-start | bytes 98308

commit v2 on v1

--- a/solution.py
+++ b/solution.py
@@ -13,13 +13,14 @@
 MOST = 8
 NEAR = 2
 Y = 4
+GROUP = 4
 MASKED = -1e30
 SCALE = HD ** -0.5
 SCALE2 = SCALE * 1.4426950408889634
 MESH = pl.DeviceIdType.MESH
 F32 = jnp.float32
 BF16 = jnp.bfloat16
-VMEM_LIMIT = 48 * 1024 * 1024
+VMEM_LIMIT = 16 * 1024 * 1024
 
 
 def dot_nt(a, b):
@@ -63,17 +64,35 @@
     return table.astype(jnp.int32)
 
 
-def stats_kernel(heads, tiles, unroll, lists_ref, counts_ref, q_ref, k_ref, v_ref, g_ref, stats_ref, table_out, table_vmem, table, sem):
+def diagonal(a, b):
+    zero = jnp.zeros_like(a)
+    return jnp.concatenate([jnp.concatenate([a, zero], axis=1), jnp.concatenate([zero, b], axis=1)], axis=0)
+
+
+def stats_kernel(heads, tiles, unroll, lists_hbm, counts_hbm, q_hbm, k_hbm, v_hbm, g_hbm,
+                 stats_ref, table_out, tops_ref, weights_ref, dprobs_ref,
+                 lists_ref, counts_ref, q_ref, k_ref, v_ref, g_ref, table, sem, table_sem):
     me = lax.axis_index("ctx")
     blocks_here = k_ref.shape[0] // BLOCK
+    fetches = [
+        pltpu.make_async_copy(source, target, sem.at[i])
+        for i, (source, target) in enumerate(
+            ((lists_hbm, lists_ref), (counts_hbm, counts_ref), (k_hbm, k_ref), (q_hbm, q_ref), (v_hbm, v_ref), (g_hbm, g_ref))
+        )
+    ]
+    for fetch in fetches:
+        fetch.start()
+    fetches[0].wait()
+    fetches[1].wait()
     for head in range(heads):
-        table_vmem[pl.ds(head * tiles, tiles), :] = slot_table(
+        table_out[pl.ds(head * tiles, tiles), :] = slot_table(
             lists_ref[head], counts_ref[pl.ds(head, 1), :], me, blocks_here
         )
-    copy = pltpu.make_async_copy(table_vmem, table, sem)
+    copy = pltpu.make_async_copy(table_out, table, table_sem)
     copy.start()
-    table_out[...] = table_vmem[...]
     copy.wait()
+    for fetch in fetches[2:]:
+        fetch.wait()
 
     def part(head, tile, first, slots):
         row = head * tiles + tile
@@ -90,149 +109,195 @@
         weights = jnp.where(mask, jnp.exp2(scores - top), 0.0)
         total = jnp.sum(weights, axis=0, keepdims=True)
         delta = jnp.sum(weights * dprobs, axis=0, keepdims=True)
-        return top, total, delta
+        return weights, dprobs, top, total, delta
 
     def near(step, carry):
         for inner in range(unroll):
             for head in range(heads):
                 tile = step * unroll + inner
                 row = head * tiles + tile
-                top, total, delta = part(head, tile, 0, NEAR)
-                stats_ref[row, pl.ds(0, 1), :] = top
-                stats_ref[row, pl.ds(1, 1), :] = total
-                stats_ref[row, pl.ds(2, 1), :] = delta
+                group = head * (tiles // GROUP) + step * (unroll // GROUP) + inner // GROUP
+                place = pl.ds(inner % GROUP, 1)
+                weights, dprobs, top, total, delta = part(head, tile, 0, NEAR)
+                weights_ref[row] = weights
+                dprobs_ref[row] = dprobs
+                tops_ref[group, place, :] = top
+                stats_ref[group, 0, place, :] = top
+                stats_ref[group, 1, place, :] = total
+                stats_ref[group, 2, place, :] = delta
         return carry
 
     lax.fori_loop(0, tiles // unroll, near, 0)
 
-    def far(tile, carry):
-        for head in range(heads):
-            row = head * tiles + tile
-
-            @pl.when(table[row, MOST] > NEAR)
-            def _():
-                top, total, delta = part(head, tile, NEAR, MOST - NEAR)
-                old = stats_ref[row, pl.ds(0, 1), :]
-                joint = jnp.maximum(old, top)
-                a = jnp.exp2(old - joint)
-                b = jnp.exp2(top - joint)
-                stats_ref[row, pl.ds(0, 1), :] = joint
-                stats_ref[row, pl.ds(1, 1), :] = a * stats_ref[row, pl.ds(1, 1), :] + b * total
-                stats_ref[row, pl.ds(2, 1), :] = a * stats_ref[row, pl.ds(2, 1), :] + b * delta
+    def far(step, carry):
+        for inner in range(GROUP):
+            for head in range(heads):
+                tile = step * GROUP + inner
+                row = head * tiles + tile
+                group = head * (tiles // GROUP) + step
+                place = pl.ds(inner, 1)
+
+                @pl.when(table[row, MOST] > NEAR)
+                def _():
+                    _, _, top, total, delta = part(head, tile, NEAR, MOST - NEAR)
+                    old = stats_ref[group, 0, place, :]
+                    joint = jnp.maximum(old, top)
+                    a = jnp.exp2(old - joint)
+                    b = jnp.exp2(top - joint)
+                    stats_ref[group, 0, place, :] = joint
+                    stats_ref[group, 1, place, :] = a * stats_ref[group, 1, place, :] + b * total
+                    stats_ref[group, 2, place, :] = a * stats_ref[group, 2, place, :] + b * delta
 
         return carry
 
-    lax.fori_loop(0, tiles, far, 0)
-
-
-def join_kernel(n, stats_ref, out_ref, recv, merged, send1, recv1, send2, recv2):
+    lax.fori_loop(0, tiles // GROUP, far, 0)
+
+
+def join_kernel(n_ctx, stats_ref, out_ref, zbuf, ybuf, part, merged, send1, recv1, send2, recv2, send3, recv3):
     me = lax.axis_index("ctx")
     head = lax.axis_index("head")
+    n_z = n_ctx // Y
+    z = me // Y
+    y = lax.rem(me, Y)
+    far_first = sorted(range(1, n_z), key=lambda i: -min(i, n_z - i))
     barrier = pltpu.get_barrier_semaphore()
-
-    def greet(step, carry):
-        peer = lax.rem(me + step, n)
-        pl.semaphore_signal(barrier, inc=1, device_id=(peer, head), device_id_type=MESH)
-        return carry
-
-    lax.fori_loop(1, n, greet, 0)
-    pl.semaphore_wait(barrier, n - 1)
-
-    def first(peer, source):
+    for i in far_first:
+        pl.semaphore_signal(barrier, inc=1, device_id=(lax.rem(z + i, n_z) * Y + y, head), device_id_type=MESH)
+    for i in range(1, Y):
+        pl.semaphore_signal(barrier, inc=1, device_id=(z * Y + lax.rem(y + i, Y), head), device_id_type=MESH)
+    pl.semaphore_wait(barrier, n_z + Y - 2)
+
+    def first(i, source):
+        peer = lax.rem(z + i, n_z)
         return pltpu.make_async_remote_copy(
-            src_ref=stats_ref.at[peer], dst_ref=recv.at[source], send_sem=send1.at[peer], recv_sem=recv1.at[source],
-            device_id=(peer, head), device_id_type=MESH,
-        )
-
-    def second(peer, source):
+            src_ref=stats_ref.at[peer], dst_ref=zbuf.at[source], send_sem=send1.at[i], recv_sem=recv1.at[source],
+            device_id=(peer * Y + y, head), device_id_type=MESH,
+        )
+
+    def second(i, source):
+        peer = lax.rem(y + i, Y)
         return pltpu.make_async_remote_copy(
-            src_ref=merged.at[source], dst_ref=merged.at[source], send_sem=send2.at[peer], recv_sem=recv2.at[source],
-            device_id=(peer, head), device_id_type=MESH,
-        )
-
-    def over(body):
-        def step(i, carry):
-            body(lax.rem(me + i, n))
-            return carry
-
-        lax.fori_loop(1, n, step, 0)
-
-    over(lambda peer: first(peer, me).start())
-    recv[me] = stats_ref[me]
-    over(lambda peer: first(peer, peer).wait_recv())
-    pieces = recv[...]
-    tops = pieces[:, 0, :]
-    top = jnp.max(tops, axis=0, keepdims=True)
-    share = jnp.exp2(tops - top)
-    total = jnp.sum(share * pieces[:, 1, :], axis=0, keepdims=True)
-    delta = jnp.sum(share * pieces[:, 2, :], axis=0, keepdims=True)
-    merged[me, pl.ds(0, 1), :] = top + jnp.log2(total)
-    merged[me, pl.ds(1, 1), :] = delta / total
-    over(lambda peer: second(peer, me).start())
-    over(lambda peer: first(peer, me).wait_send())
-    over(lambda peer: second(peer, peer).wait_recv())
+            src_ref=part, dst_ref=ybuf.at[source], send_sem=send2.at[i], recv_sem=recv2.at[source],
+            device_id=(z * Y + peer, head), device_id_type=MESH,
+        )
+
+    def third(i, source):
+        peer = lax.rem(z + i, n_z)
+        return pltpu.make_async_remote_copy(
+            src_ref=merged.at[source], dst_ref=merged.at[source], send_sem=send3.at[i], recv_sem=recv3.at[source],
+            device_id=(peer * Y + y, head), device_id_type=MESH,
+        )
+
+    def combine(pieces):
+        tops = pieces[:, 0]
+        top = jnp.max(tops, axis=0)
+        share = jnp.exp2(tops - top[None])
+        return top, jnp.sum(share * pieces[:, 1], axis=0), jnp.sum(share * pieces[:, 2], axis=0)
+
+    for i in far_first:
+        first(i, z).start()
+    zbuf[z] = stats_ref[z]
+    for i in range(1, n_z):
+        first(i, lax.rem(z + i, n_z)).wait_recv()
+    for kind, value in enumerate(combine(zbuf[...])):
+        part[kind] = value
+    for i in (2, 1, 3):
+        second(i, y).start()
+    ybuf[y] = part[...]
+    for i in range(1, Y):
+        second(i, lax.rem(y + i, Y)).wait_recv()
+    top, total, delta = combine(ybuf[...])
+    merged[z, 0] = top + jnp.log2(total)
+    merged[z, 1] = delta / total
+    for i in far_first:
+        third(i, z).start()
+    for i in range(1, n_z):
+        first(i, z).wait_send()
+    for i in range(1, Y):
+        second(i, y).wait_send()
+    for i in range(1, n_z):
+        third(i, lax.rem(z + i, n_z)).wait_recv()
     out_ref[...] = merged[...]
-    over(lambda peer: second(peer, me).wait_send())
-
-
-def grads_kernel(heads, tiles, unroll, table, stats_ref, q_ref, k_ref, v_ref, g_ref, dq_ref, dk_ref, dv_ref, dk_acc, dv_acc):
-    dk_acc[...] = jnp.zeros_like(dk_acc)
-    dv_acc[...] = jnp.zeros_like(dv_acc)
-
-    def part(head, tile, first, slots):
+    for i in range(1, n_z):
+        third(i, z).wait_send()
+
+
+def grads_kernel(heads, tiles, unroll, table, totals_ref, tops_ref, weights_ref, dprobs_ref, q_ref, k_ref, v_ref, g_ref,
+                 dq_ref, dk_ref, dv_ref, acc):
+    acc[...] = jnp.zeros_like(acc)
+
+    def spread(head, tile, group, place, first, probs, dprobs, keys):
         row = head * tiles + tile
-        live = (table[row, MOST] - first) * BLOCK
         rows = pl.ds(pl.multiple_of(tile * TILE, TILE), TILE)
         cols = pl.ds(head * HD, HD)
-        keys = picked(k_ref, table, row, head, first, slots)
-        vals = picked(v_ref, table, row, head, first, slots)
-        query = q_ref[rows, cols]
-        grad = g_ref[rows, cols]
-        scores = dot_nt(keys, query) * SCALE2
-        dprobs = dot_nt(vals, grad)
-        mask = lax.broadcasted_iota(jnp.int32, scores.shape, 0) < live
-        log_total = stats_ref[row, pl.ds(0, 1), :]
-        delta = stats_ref[row, pl.ds(1, 1), :]
-        probs = jnp.where(mask, jnp.exp2(scores - log_total), 0.0)
-        dscores = (probs * (dprobs - delta)).astype(BF16)
-        low = probs.astype(BF16)
-        dkeys = dot_nn(dscores, query)
-        dvals = dot_nn(low, grad)
-        dquery = dot_tn(dscores, keys) * SCALE
-        for slot in range(slots):
+        dscores = (probs * (dprobs - totals_ref[group, 1, place, :])).astype(BF16)
+        both = jnp.concatenate([dscores, probs.astype(BF16)], axis=1)
+        moved = dot_nn(both, diagonal(q_ref[rows, cols], g_ref[rows, cols]))
+        for slot in range(keys.shape[0] // BLOCK):
             start = pl.multiple_of(table[row, first + slot] * BLOCK, BLOCK)
-            dk_acc[head, pl.ds(start, BLOCK), :] += dkeys[slot * BLOCK : (slot + 1) * BLOCK]
-            dv_acc[head, pl.ds(start, BLOCK), :] += dvals[slot * BLOCK : (slot + 1) * BLOCK]
-        return dquery
+            acc[head, pl.ds(start, BLOCK), :] += moved[slot * BLOCK : (slot + 1) * BLOCK]
+        return dscores
 
     def near(step, carry):
         for inner in range(unroll):
+            tile = step * unroll + inner
+            rows = pl.ds(pl.multiple_of(tile * TILE, TILE), TILE)
+            place = pl.ds(inner % GROUP, 1)
+            pieces = []
             for head in range(heads):
-                tile = step * unroll + inner
-                rows = pl.ds(pl.multiple_of(tile * TILE, TILE), TILE)
-                dq_ref[rows, pl.ds(head * HD, HD)] = part(head, tile, 0, NEAR).astype(BF16)
+                row = head * tiles + tile
+                group = head * (tiles // GROUP) + step * (unroll // GROUP) + inner // GROUP
+                share = jnp.exp2(tops_ref[group, place, :] - totals_ref[group, 0, place, :])
+                keys = picked(k_ref, table, row, head, 0, NEAR)
+                dscores = spread(head, tile, group, place, 0, weights_ref[row] * share, dprobs_ref[row], keys)
+                pieces.append((dscores, keys))
+            moved = dot_tn(
+                jnp.concatenate([pieces[0][0], pieces[1][0]], axis=0), diagonal(pieces[0][1], pieces[1][1])
+            )
+            dq_ref[rows, :] = (moved * SCALE).astype(BF16)
         return carry
 
     lax.fori_loop(0, tiles // unroll, near, 0)
 
-    def far(tile, carry):
-        for head in range(heads):
-            row = head * tiles + tile
-
-            @pl.when(table[row, MOST] > NEAR)
-            def _():
-                rows = pl.ds(pl.multiple_of(tile * TILE, TILE), TILE)
-                cols = pl.ds(head * HD, HD)
-                extra = part(head, tile, NEAR, MOST - NEAR)
-                dq_ref[rows, cols] = (dq_ref[rows, cols].astype(F32) + extra).astype(BF16)
+    def far(step, carry):
+        for inner in range(GROUP):
+            for head in range(heads):
+                tile = step * GROUP + inner
+                row = head * tiles + tile
+                group = head * (tiles // GROUP) + step
+                place = pl.ds(inner, 1)
+
+                @pl.when(table[row, MOST] > NEAR)
+                def _():
+                    rows = pl.ds(pl.multiple_of(tile * TILE, TILE), TILE)
+                    cols = pl.ds(head * HD, HD)
+                    live = (table[row, MOST] - NEAR) * BLOCK
+                    keys = picked(k_ref, table, row, head, NEAR, MOST - NEAR)
+                    vals = picked(v_ref, table, row, head, NEAR, MOST - NEAR)
+                    scores = dot_nt(keys, q_ref[rows, cols]) * SCALE2
+                    dprobs = dot_nt(vals, g_ref[rows, cols])
+                    mask = lax.broadcasted_iota(jnp.int32, scores.shape, 0) < live
+                    probs = jnp.where(mask, jnp.exp2(scores - totals_ref[group, 0, place, :]), 0.0)
+                    dscores = spread(head, tile, group, place, NEAR, probs, dprobs, keys)
+                    extra = dot_tn(dscores, keys) * SCALE
+                    dq_ref[rows, cols] = (dq_ref[rows, cols].astype(F32) + extra).astype(BF16)
 
         return carry
 
-    lax.fori_loop(0, tiles, far, 0)
+    lax.fori_loop(0, tiles // GROUP, far, 0)
     for head in range(heads):
         cols = pl.ds(head * HD, HD)
-        dk_ref[:, cols] = (dk_acc[head] * SCALE).astype(BF16)
-        dv_ref[:, cols] = dv_acc[head].astype(BF16)
+        dk_ref[:, cols] = (acc[head, :, pl.ds(0, HD)] * SCALE).astype(BF16)
+        dv_ref[:, cols] = acc[head, :, pl.ds(HD, HD)].astype(BF16)
+
+
+def leave_kernel(count, *refs):
+    sem = refs[2 * count]
+    copies = [pltpu.make_async_copy(refs[i], refs[count + i], sem.at[i]) for i in range(count)]
+    for copy in copies:
+        copy.start()
+    for copy in copies:
+        copy.wait()
 
 
 def swap_kernel(n_ctx, n_head, dq_ref, dk_ref, dv_ref, oq_ref, ok_ref, ov_ref,
@@ -345,31 +410,51 @@
     own = latents // n_ctx
     vmem = pl.BlockSpec(memory_space=pltpu.VMEM)
     smem = pl.BlockSpec(memory_space=pltpu.SMEM)
-    anyplace = pl.BlockSpec(memory_space=pl.ANY)
-    stats, table = pl.pallas_call(
+    hbm = pl.BlockSpec(memory_space=pltpu.HBM)
+    stats, table, tops, weights, dprobs = pl.pallas_call(
         functools.partial(stats_kernel, heads, tiles, 4),
         name="local_stats",
-        out_shape=(jax.ShapeDtypeStruct((rows, 3, TILE), F32), jax.ShapeDtypeStruct((rows, 128), jnp.int32)),
-        in_specs=[vmem] * 6,
-        out_specs=(vmem, vmem),
-        scratch_shapes=[pltpu.VMEM((rows, 128), jnp.int32), pltpu.SMEM((rows, 128), jnp.int32), pltpu.SemaphoreType.DMA],
+        out_shape=(
+            jax.ShapeDtypeStruct((n_z, 3, GROUP, TILE), F32),
+            jax.ShapeDtypeStruct((rows, 128), jnp.int32),
+            jax.ShapeDtypeStruct((n_z, GROUP, TILE), F32),
+            jax.ShapeDtypeStruct((rows, NEAR * BLOCK, TILE), F32),
+            jax.ShapeDtypeStruct((rows, NEAR * BLOCK, TILE), F32),
+        ),
+        in_specs=[hbm] * 6,
+        out_specs=(vmem,) * 5,
+        scratch_shapes=[
+            pltpu.VMEM(block_lists.shape, jnp.int32),
+            pltpu.VMEM(list_counts.shape, jnp.int32),
+            pltpu.VMEM(queries.shape, BF16),
+            pltpu.VMEM(prefix_keys.shape, BF16),
+            pltpu.VMEM(prefix_values.shape, BF16),
+            pltpu.VMEM(out_grad.shape, BF16),
+            pltpu.SMEM((rows, 128), jnp.int32),
+            pltpu.SemaphoreType.DMA((6,)),
+            pltpu.SemaphoreType.DMA,
+        ],
         compiler_params=pltpu.CompilerParams(vmem_limit_bytes=VMEM_LIMIT),
-    )(block_lists, list_counts, queries, prefix_keys, prefix_values, out_grad)
+    )(*[pltpu.with_memory_space_constraint(x, pltpu.HBM) for x in (block_lists, list_counts, queries, prefix_keys, prefix_values, out_grad)])
     totals = pl.pallas_call(
         functools.partial(join_kernel, n_ctx),
         name="join_stats",
-        out_shape=jax.ShapeDtypeStruct((rows, 2, TILE), F32),
+        out_shape=jax.ShapeDtypeStruct((n_z, 2, GROUP, TILE), F32),
         in_specs=[vmem],
         out_specs=vmem,
         scratch_shapes=[
-            pltpu.VMEM((n_ctx, 3, TILE), F32),
-            pltpu.VMEM((n_ctx, 2, TILE), F32),
-            pltpu.SemaphoreType.DMA((n_ctx,)),
-            pltpu.SemaphoreType.DMA((n_ctx,)),
-            pltpu.SemaphoreType.DMA((n_ctx,)),
-            pltpu.SemaphoreType.DMA((n_ctx,)),
+            pltpu.VMEM((n_z, 3, GROUP, TILE), F32),
+            pltpu.VMEM((Y, 3, GROUP, TILE), F32),
+            pltpu.VMEM((3, GROUP, TILE), F32),
+            pltpu.VMEM((n_z, 2, GROUP, TILE), F32),
+            pltpu.SemaphoreType.DMA((n_z,)),
+            pltpu.SemaphoreType.DMA((n_z,)),
+            pltpu.SemaphoreType.DMA((Y,)),
+            pltpu.SemaphoreType.DMA((Y,)),
+            pltpu.SemaphoreType.DMA((n_z,)),
+            pltpu.SemaphoreType.DMA((n_z,)),
         ],
-        compiler_params=pltpu.CompilerParams(collective_id=0, has_side_effects=True),
+        compiler_params=pltpu.CompilerParams(collective_id=0, has_side_effects=True, vmem_limit_bytes=VMEM_LIMIT),
     )(stats)
     dq, dk, dv = pl.pallas_call(
         functools.partial(grads_kernel, heads, tiles, 4),
@@ -379,13 +464,13 @@
             jax.ShapeDtypeStruct((tokens, width), BF16),
             jax.ShapeDtypeStruct((tokens, width), BF16),
         ),
-        in_specs=[smem] + [vmem] * 5,
+        in_specs=[smem] + [vmem] * 8,
         out_specs=(vmem, vmem, vmem),
-        scratch_shapes=[pltpu.VMEM((heads, tokens, HD), F32), pltpu.VMEM((heads, tokens, HD), F32)],
+        scratch_shapes=[pltpu.VMEM((heads, tokens, 2 * HD), F32)],
         compiler_params=pltpu.CompilerParams(vmem_limit_bytes=VMEM_LIMIT),
-    )(table, totals, queries, prefix_keys, prefix_values, out_grad)
+    )(table, totals, tops, weights, dprobs, queries, prefix_keys, prefix_values, out_grad)
     piece = tokens // n_head
-    return pl.pallas_call(
+    results = pl.pallas_call(
         functools.partial(swap_kernel, n_ctx, n_head),
         name="swap_grads",
         out_shape=(
@@ -409,6 +494,15 @@
         ],
         compiler_params=pltpu.CompilerParams(collective_id=1, has_side_effects=True, vmem_limit_bytes=VMEM_LIMIT),
     )(dq.reshape(n_z, Y, own, width), dk, dv)
+    return pl.pallas_call(
+        functools.partial(leave_kernel, len(results)),
+        name="leave",
+        out_shape=tuple(jax.ShapeDtypeStruct(result.shape, result.dtype) for result in results),
+        in_specs=[vmem] * len(results),
+        out_specs=(hbm,) * len(results),
+        scratch_shapes=[pltpu.SemaphoreType.DMA((len(results),))],
+        compiler_params=pltpu.CompilerParams(vmem_limit_bytes=VMEM_LIMIT),
+    )(*results)
 
 
 def solution(mesh):

time: 69.5 us -> 52.4 us (0.75)
  local copies, waits for them, and re-layouts: 9.51 us -> 0.02 us
  Pallas kernels: 58.8 us -> 51.6 us
    unnamed x27 -> x8, local copies, waits for them, and re-layouts: 9.51 us -> 0.02 us
    pallas_call x1, Pallas kernels: 9.74 us -> 3.42 us  [local(): pl.pallas_call(functools.partial(grads_kernel, heads, tiles, 4), name='lo...]
    pallas_call x1, Pallas kernels: 23 us -> 19.9 us  [local(): pl.pallas_call(functools.partial(join_kernel, n_ctx), name='join_stats',...]
    pallas_call x0 -> x1, Pallas kernels: none -> 1.01 us  [local(): pl.pallas_call(functools.partial(leave_kernel, len(results)), name='leave...]
where the time goes in v2:
time: 52.4 us; the launch traced here: 52.3 us
  Pallas kernels  51.6 us (98%)
  between operations  0.73 us (1%)
    pallas_call x1, Pallas kernels, local(): pl.pallas_call(functools.partial(swap_kernel, n_ctx, n_head), name='swap_...  22.4 us
    pallas_call x1, Pallas kernels, local(): pl.pallas_call(functools.partial(join_kernel, n_ctx), name='join_stats',...  19.9 us
    pallas_call x1, Pallas kernels, local(): pl.pallas_call(functools.partial(stats_kernel, heads, tiles, 4), name='lo...  4.84 us
    pallas_call x1, Pallas kernels, local(): pl.pallas_call(functools.partial(grads_kernel, heads, tiles, 4), name='lo...  3.42 us

profile of v2, /device:TPU:1, one launch (start us, length us, event | category | flops | bytes accessed | tf_op | source)
XLA Modules:
  0.0 52.3 jit_solution(103676946660935052)
XLA Ops:
  0.6 0.0 copy-start.1
  0.6 0.0 copy-start.3
  0.7 0.0 copy-start.2
  0.7 0.0 copy-start
  0.7 4.8 %local_stats.1 = (f32[8,3,4,128]{3,2,1,0:T(4,128)S(1)}, s32[32,128]{1,0:T(8,128)S(1)}, f32[8,4,128]{2,1,0:T(4,128)S(1)}, f32[32,128,128]{2,1,0:T(8,128)S(1)}, f32[32,128,128]{2,1,0:T(8,128)S(1)}) custom-call(s32[2,16,64]{2,1,0:T(8,128)} %lists_hbm.1, s32[2,16]{1,0:T(2,128)} %counts_hbm.1, bf16[2048,256]{1,0:T(8,128)(2,1)} %q_ref.1, bf16[1024,256]{1,0:T(8,128)(2,1)} %k_ref.1, ...), custom_call_target="tpu_custom_call" | custom-call | tf_op jit(solution)/shard_map/local_stats/pallas_call | solution.py:414
  5.5 19.9 %join_stats.1.totals_ref = f32[8,2,4,128]{3,2,1,0:T(4,128)S(1)} custom-call(f32[8,3,4,128]{3,2,1,0:T(4,128)S(1)} %get-tuple-element.15.stats_ref), custom_call_target="tpu_custom_call" | custom-call | tf_op jit(solution)/shard_map/join_stats/pallas_call | solution.py:439
  25.5 0.0 copy-done.1
  25.5 0.0 copy-done.3
  25.5 0.0 copy-done.2
  25.5 0.0 copy-done
  25.5 3.4 %local_grads.1 = (bf16[2048,256]{1,0:T(8,128)(2,1)S(1)}, bf16[1024,256]{1,0:T(8,128)(2,1)S(1)}, bf16[1024,256]{1,0:T(8,128)(2,1)S(1)}) custom-call(s32[32,128]{1,0:T(8,128)S(1)} %get-tuple-element.14.table, f32[8,2,4,128]{3,2,1,0:T(4,128)S(1)} %join_stats.1.totals_ref, f32[8,4,128]{2,1,0:T(4,128)S(1)} %get-tuple-element.16.tops_ref, ...), custom_call_target="tpu_custom_call" | custom-call | tf_op jit(solution)/shard_map/local_grads/pallas_call | solution.py:459
  28.9 22.4 %swap_grads.1 = (bf16[64,256]{1,0:T(8,128)(2,1)S(1)}, bf16[128,2048]{1,0:T(8,128)(2,1)S(1)}, bf16[128,2048]{1,0:T(8,128)(2,1)S(1)}) custom-call(bf16[8,4,64,256]{3,2,1,0:T(8,128)(2,1)S(1)} %bitcast.1, bf16[1024,256]{1,0:T(8,128)(2,1)S(1)} %get-tuple-element.20.dk_ref, bf16[1024,256]{1,0:T(8,128)(2,1)S(1)} %get-tuple-element.21.dv_ref), custom_call_target="tpu_custom_call" | custom-call | tf_op jit(solution)/shard_map/swap_grads/pallas_call | solution.py:473
  51.3 1.0 %leave.1 = (bf16[64,256]{1,0:T(8,128)(2,1)}, bf16[128,2048]{1,0:T(8,128)(2,1)}, bf16[128,2048]{1,0:T(8,128)(2,1)}) custom-call(bf16[64,256]{1,0:T(8,128)(2,1)S(1)} %get-tuple-element.22.refs_0_, bf16[128,2048]{1,0:T(8,128)(2,1)S(1)} %get-tuple-element.23.refs_1_, bf16[128,2048]{1,0:T(8,128)(2,1)S(1)} %get-tuple-element.24.refs_2_), custom_call_target="tpu_custom_call" | custom-call | tf_op jit(solution)/shard_map/leave/pallas_call | solution.py:497
Async XLA Ops:
  0.6 24.8 %copy-start.1 = (bf16[2048,256]{1,0:T(8,128)(2,1)S(1)}, bf16[2048,256]{1,0:T(8,128)(2,1)}, u32[]{:S(2)}) copy-start(bf16[2048,256]{1,0:T(8,128)(2,1)} %g_ref.1) | copy-start | bytes 3145732
  0.6 24.8 %copy-start.3 = (bf16[1024,256]{1,0:T(8,128)(2,1)S(1)}, bf16[1024,256]{1,0:T(8,128)(2,1)}, u32[]{:S(2)}) copy-start(bf16[1024,256]{1,0:T(8,128)(2,1)} %v_ref.1) | copy-start | bytes 1572868
  0.7 24.8 %copy-start.2 = (bf16[1024,256]{1,0:T(8,128)(2,1)S(1)}, bf16[1024,256]{1,0:T(8,128)(2,1)}, u32[]{:S(2)}) copy-start(bf16[1024,256]{1,0:T(8,128)(2,1)} %k_ref.1) | copy-start | bytes 1572868
  0.7 24.8 %copy-start = (bf16[2048,256]{1,0:T(8,128)(2,1)S(1)}, bf16[2048,256]{1,0:T(8,128)(2,1)}, u32[]{:S(2)}) copy-start(bf16[2048,256]{1,0:T(8,128)(2,1)} %q_ref.1) | copy-start | bytes 3145732

commit v3 on v2

--- a/solution.py
+++ b/solution.py
@@ -14,6 +14,8 @@
 NEAR = 2
 Y = 4
 GROUP = 4
+LATE = 16
+LATE_AFTER = 5
 MASKED = -1e30
 SCALE = HD ** -0.5
 SCALE2 = SCALE * 1.4426950408889634
@@ -223,7 +225,7 @@
 
 
 def grads_kernel(heads, tiles, unroll, table, totals_ref, tops_ref, weights_ref, dprobs_ref, q_ref, k_ref, v_ref, g_ref,
-                 dq_ref, dk_ref, dv_ref, acc):
+                 dq_ref, acc):
     acc[...] = jnp.zeros_like(acc)
 
     def spread(head, tile, group, place, first, probs, dprobs, keys):
@@ -285,10 +287,6 @@
         return carry
 
     lax.fori_loop(0, tiles // GROUP, far, 0)
-    for head in range(heads):
-        cols = pl.ds(head * HD, HD)
-        dk_ref[:, cols] = (acc[head, :, pl.ds(0, HD)] * SCALE).astype(BF16)
-        dv_ref[:, cols] = acc[head, :, pl.ds(HD, HD)].astype(BF16)
 
 
 def leave_kernel(count, *refs):
@@ -300,8 +298,9 @@
         copy.wait()
 
 
-def swap_kernel(n_ctx, n_head, dq_ref, dk_ref, dv_ref, oq_ref, ok_ref, ov_ref,
-                ybuf, zsend, zbuf, ssend, srecv, ysend, yrecv, zsend_sem, zrecv, own):
+def swap_kernel(n_ctx, n_head, dq_ref, acc_ref, oq_ref, ok_ref, ov_ref, dk_ref, dv_ref,
+                ybuf, zsend, zbuf, late_zbuf, late_send, late_ybuf,
+                ssend, srecv, ysend, yrecv, zsend_sem, zrecv, late_zsend, late_zrecv, late_ysend, late_yrecv, own):
     me = lax.axis_index("ctx")
     head = lax.axis_index("head")
     n_z = n_ctx // Y
@@ -309,6 +308,13 @@
     y = lax.rem(me, Y)
     tokens = ok_ref.shape[0]
     width = dk_ref.shape[1]
+    late = late_send.shape[1]
+    early = oq_ref.shape[0] - late
+    first_rows = pl.ds(0, early)
+    last_rows = pl.ds(early, late)
+    far_first = sorted(range(1, n_z), key=lambda i: -min(i, n_z - i))
+    far_heads = sorted(range(1, n_head), key=lambda i: -min(i, n_head - i))
+    order = far_first + [0]
     barrier = pltpu.get_barrier_semaphore()
 
     def at_head(i):
@@ -320,9 +326,13 @@
     def at_z(i):
         return (lax.rem(z + i, n_z) * Y + y, head)
 
-    for count, where in ((n_head, at_head), (Y, at_y), (n_z, at_z)):
+    for count, where in ((n_z, at_z), (n_head, at_head), (Y, at_y)):
         for i in range(1, count):
             pl.semaphore_signal(barrier, inc=1, device_id=where(i), device_id_type=MESH)
+    for part in range(acc_ref.shape[0]):
+        cols = pl.ds(part * HD, HD)
+        dk_ref[:, cols] = (acc_ref[part, :, pl.ds(0, HD)] * SCALE).astype(BF16)
+        dv_ref[:, cols] = acc_ref[part, :, pl.ds(HD, HD)].astype(BF16)
     pl.semaphore_wait(barrier, n_head + Y + n_z - 3)
 
     def token_copy(which, i, source):
@@ -338,7 +348,7 @@
     def y_copy(zz, i, source):
         peer = lax.rem(y + i, Y)
         return pltpu.make_async_remote_copy(
-            src_ref=dq_ref.at[zz, peer], dst_ref=ybuf.at[zz, source],
+            src_ref=dq_ref.at[zz, peer, first_rows], dst_ref=ybuf.at[zz, source],
             send_sem=ysend.at[zz, i], recv_sem=yrecv.at[zz, source],
             device_id=(z * Y + peer, head), device_id_type=MESH,
         )
@@ -351,13 +361,31 @@
             device_id=(peer * Y + y, head), device_id_type=MESH,
         )
 
-    for i in range(1, n_z + 1):
+    def late_z_copy(i, source):
+        peer = lax.rem(z + i, n_z)
+        return pltpu.make_async_remote_copy(
+            src_ref=dq_ref.at[peer, :, last_rows], dst_ref=late_zbuf.at[source],
+            send_sem=late_zsend.at[i], recv_sem=late_zrecv.at[source],
+            device_id=(peer * Y + y, head), device_id_type=MESH,
+        )
+
+    def late_y_copy(i, source):
+        peer = lax.rem(y + i, Y)
+        return pltpu.make_async_remote_copy(
+            src_ref=late_send.at[peer], dst_ref=late_ybuf.at[source],
+            send_sem=late_ysend.at[i], recv_sem=late_yrecv.at[source],
+            device_id=(z * Y + peer, head), device_id_type=MESH,
+        )
+
+    for i in far_heads:
+        for which in range(2):
+            token_copy(which, i, head).start()
+    for i in far_first:
+        late_z_copy(i, z).start()
+    for i in order:
         zz = lax.rem(z + i, n_z)
         for j in (2, 1, 3):
             y_copy(zz, j, y).start()
-    for i in range(1, n_head):
-        for which in range(2):
-            token_copy(which, i, head).start()
     mine = []
     for which in range(2):
         src, dst = ((dk_ref, ok_ref), (dv_ref, ov_ref))[which]
@@ -369,32 +397,50 @@
         copy.start()
         mine.append(copy)
 
-    for i in range(1, n_z + 1):
+    for count, i in enumerate(order):
         zz = lax.rem(z + i, n_z)
-        total = dq_ref[zz, y].astype(F32)
+        total = dq_ref[zz, y, first_rows].astype(F32)
         for j in range(1, Y):
             source = lax.rem(y + j, Y)
             y_copy(zz, j, source).wait_recv()
             total = total + ybuf[zz, source].astype(F32)
-        if i < n_z:
+        if i > 0:
             zsend[zz] = total.astype(BF16)
             z_copy(i, z).start()
+        if count == LATE_AFTER:
+            crossed = dq_ref[z, :, last_rows].astype(F32)
+            for j in range(1, n_z):
+                source = lax.rem(z + j, n_z)
+                late_z_copy(j, source).wait_recv()
+                crossed = crossed + late_zbuf[source].astype(F32)
+            late_send[...] = crossed.astype(BF16)
+            for j in (2, 1, 3):
+                late_y_copy(j, y).start()
     for i in range(1, n_z):
         source = lax.rem(z + i, n_z)
         z_copy(i, source).wait_recv()
         total = total + zbuf[source].astype(F32)
-    oq_ref[...] = total.astype(BF16)
+    oq_ref[first_rows, :] = total.astype(BF16)
+    total = late_send[y].astype(F32)
+    for j in range(1, Y):
+        source = lax.rem(y + j, Y)
+        late_y_copy(j, source).wait_recv()
+        total = total + late_ybuf[source].astype(F32)
+    oq_ref[last_rows, :] = total.astype(BF16)
     for copy in mine:
         copy.wait()
     for i in range(1, n_head):
         for which in range(2):
             token_copy(which, i, lax.rem(head + i, n_head)).wait_recv()
-    for i in range(1, n_z + 1):
+    for i in order:
         zz = lax.rem(z + i, n_z)
         for j in range(1, Y):
             y_copy(zz, j, y).wait_send()
     for i in range(1, n_z):
         z_copy(i, z).wait_send()
+        late_z_copy(i, z).wait_send()
+    for i in range(1, Y):
+        late_y_copy(i, y).wait_send()
     for i in range(1, n_head):
         for which in range(2):
             token_copy(which, i, head).wait_send()
@@ -456,17 +502,15 @@
         ],
         compiler_params=pltpu.CompilerParams(collective_id=0, has_side_effects=True, vmem_limit_bytes=VMEM_LIMIT),
     )(stats)
-    dq, dk, dv = pl.pallas_call(
+    dq, acc = pl.pallas_call(
         functools.partial(grads_kernel, heads, tiles, 4),
         name="local_grads",
         out_shape=(
             jax.ShapeDtypeStruct((latents, width), BF16),
-            jax.ShapeDtypeStruct((tokens, width), BF16),
-            jax.ShapeDtypeStruct((tokens, width), BF16),
+            jax.ShapeDtypeStruct((heads, tokens, 2 * HD), F32),
         ),
         in_specs=[smem] + [vmem] * 8,
-        out_specs=(vmem, vmem, vmem),
-        scratch_shapes=[pltpu.VMEM((heads, tokens, 2 * HD), F32)],
+        out_specs=(vmem, vmem),
         compiler_params=pltpu.CompilerParams(vmem_limit_bytes=VMEM_LIMIT),
     )(table, totals, tops, weights, dprobs, queries, prefix_keys, prefix_values, out_grad)
     piece = tokens // n_head
@@ -478,22 +522,31 @@
             jax.ShapeDtypeStruct((piece, n_head * width), BF16),
             jax.ShapeDtypeStruct((piece, n_head * width), BF16),
         ),
-        in_specs=[vmem, vmem, vmem],
+        in_specs=[vmem, vmem],
         out_specs=(vmem, vmem, vmem),
         scratch_shapes=[
-            pltpu.VMEM((n_z, Y, own, width), BF16),
-            pltpu.VMEM((n_z, own, width), BF16),
-            pltpu.VMEM((n_z, own, width), BF16),
+            pltpu.VMEM((tokens, width), BF16),
+            pltpu.VMEM((tokens, width), BF16),
+            pltpu.VMEM((n_z, Y, own - LATE, width), BF16),
+            pltpu.VMEM((n_z, own - LATE, width), BF16),
+            pltpu.VMEM((n_z, own - LATE, width), BF16),
+            pltpu.VMEM((n_z, Y, LATE, width), BF16),
+            pltpu.VMEM((Y, LATE, width), BF16),
+            pltpu.VMEM((Y, LATE, width), BF16),
             pltpu.SemaphoreType.DMA((2, n_head)),
             pltpu.SemaphoreType.DMA((2, n_head)),
             pltpu.SemaphoreType.DMA((n_z, Y)),
             pltpu.SemaphoreType.DMA((n_z, Y)),
             pltpu.SemaphoreType.DMA((n_z,)),
             pltpu.SemaphoreType.DMA((n_z,)),
+            pltpu.SemaphoreType.DMA((n_z,)),
+            pltpu.SemaphoreType.DMA((n_z,)),
+            pltpu.SemaphoreType.DMA((Y,)),
+            pltpu.SemaphoreType.DMA((Y,)),
             pltpu.SemaphoreType.DMA((2,)),
         ],
         compiler_params=pltpu.CompilerParams(collective_id=1, has_side_effects=True, vmem_limit_bytes=VMEM_LIMIT),
-    )(dq.reshape(n_z, Y, own, width), dk, dv)
+    )(dq.reshape(n_z, Y, own, width), acc)
     return pl.pallas_call(
         functools.partial(leave_kernel, len(results)),
         name="leave",

time: 52.4 us -> 50.3 us (0.960)
  Pallas kernels: 51.6 us -> 49.5 us
    pallas_call x1, Pallas kernels: 22.4 us -> 20.3 us  [local(): pl.pallas_call(functools.partial(swap_kernel, n_ctx, n_head), name='swap_...]
where the time goes in v3:
time: 50.3 us
  Pallas kernels  49.5 us (98%)
  between operations  0.73 us (1%)
    pallas_call x1, Pallas kernels, local(): pl.pallas_call(functools.partial(swap_kernel, n_ctx, n_head), name='swap_...  20.3 us
    pallas_call x1, Pallas kernels, local(): pl.pallas_call(functools.partial(join_kernel, n_ctx), name='join_stats',...  19.5 us
    pallas_call x1, Pallas kernels, local(): pl.pallas_call(functools.partial(stats_kernel, heads, tiles, 4), name='lo...  5.13 us
    pallas_call x1, Pallas kernels, local(): pl.pallas_call(functools.partial(grads_kernel, heads, tiles, 4), name='lo...  3.66 us

profile of v3, /device:TPU:1, one launch (start us, length us, event | category | flops | bytes accessed | tf_op | source)
XLA Modules:
  0.0 50.3 jit_solution(15273373323730166753)
XLA Ops:
  0.6 0.0 copy-start.1
  0.6 0.0 copy-start.3
  0.7 0.0 copy-start.2
  0.7 0.0 copy-start
  0.7 5.1 %local_stats.1 = (f32[8,3,4,128]{3,2,1,0:T(4,128)S(1)}, s32[32,128]{1,0:T(8,128)S(1)}, f32[8,4,128]{2,1,0:T(4,128)S(1)}, f32[32,128,128]{2,1,0:T(8,128)S(1)}, f32[32,128,128]{2,1,0:T(8,128)S(1)}) custom-call(s32[2,16,64]{2,1,0:T(8,128)} %lists_hbm.1, s32[2,16]{1,0:T(2,128)} %counts_hbm.1, bf16[2048,256]{1,0:T(8,128)(2,1)} %q_ref.1, bf16[1024,256]{1,0:T(8,128)(2,1)} %k_ref.1, ...), custom_call_target="tpu_custom_call" | custom-call | tf_op jit(solution)/shard_map/local_stats/pallas_call | solution.py:460
  5.8 19.5 %join_stats.1.totals_ref = f32[8,2,4,128]{3,2,1,0:T(4,128)S(1)} custom-call(f32[8,3,4,128]{3,2,1,0:T(4,128)S(1)} %get-tuple-element.14.stats_ref), custom_call_target="tpu_custom_call" | custom-call | tf_op jit(solution)/shard_map/join_stats/pallas_call | solution.py:485
  25.3 0.0 copy-done.1
  25.3 0.0 copy-done.3
  25.3 0.0 copy-done.2
  25.3 0.0 copy-done
  25.3 3.7 %local_grads.1 = (bf16[2048,256]{1,0:T(8,128)(2,1)S(1)}, f32[2,1024,256]{2,1,0:T(8,128)S(1)}) custom-call(s32[32,128]{1,0:T(8,128)S(1)} %get-tuple-element.13.table, f32[8,2,4,128]{3,2,1,0:T(4,128)S(1)} %join_stats.1.totals_ref, f32[8,4,128]{2,1,0:T(4,128)S(1)} %get-tuple-element.15.tops_ref, f32[32,128,128]{2,1,0:T(8,128)S(1)} %get-tuple-element.16.weights_ref, ...), custom_call_target="tpu_custom_call" | custom-call | tf_op jit(solution)/shard_map/local_grads/pallas_call | solution.py:505
  29.0 20.3 %swap_grads.1 = (bf16[64,256]{1,0:T(8,128)(2,1)S(1)}, bf16[128,2048]{1,0:T(8,128)(2,1)S(1)}, bf16[128,2048]{1,0:T(8,128)(2,1)S(1)}) custom-call(bf16[8,4,64,256]{3,2,1,0:T(8,128)(2,1)S(1)} %bitcast.1, f32[2,1024,256]{2,1,0:T(8,128)S(1)} %get-tuple-element.19.acc_ref), custom_call_target="tpu_custom_call" | custom-call | tf_op jit(solution)/shard_map/swap_grads/pallas_call | solution.py:517
  49.3 1.0 %leave.1 = (bf16[64,256]{1,0:T(8,128)(2,1)}, bf16[128,2048]{1,0:T(8,128)(2,1)}, bf16[128,2048]{1,0:T(8,128)(2,1)}) custom-call(bf16[64,256]{1,0:T(8,128)(2,1)S(1)} %get-tuple-element.20.refs_0_, bf16[128,2048]{1,0:T(8,128)(2,1)S(1)} %get-tuple-element.21.refs_1_, bf16[128,2048]{1,0:T(8,128)(2,1)S(1)} %get-tuple-element.22.refs_2_), custom_call_target="tpu_custom_call" | custom-call | tf_op jit(solution)/shard_map/leave/pallas_call | solution.py:550
Async XLA Ops:
  0.6 24.7 %copy-start.1 = (bf16[2048,256]{1,0:T(8,128)(2,1)S(1)}, bf16[2048,256]{1,0:T(8,128)(2,1)}, u32[]{:S(2)}) copy-start(bf16[2048,256]{1,0:T(8,128)(2,1)} %g_ref.1) | copy-start | bytes 3145732
  0.6 24.7 %copy-start.3 = (bf16[1024,256]{1,0:T(8,128)(2,1)S(1)}, bf16[1024,256]{1,0:T(8,128)(2,1)}, u32[]{:S(2)}) copy-start(bf16[1024,256]{1,0:T(8,128)(2,1)} %v_ref.1) | copy-start | bytes 1572868
  0.7 24.7 %copy-start.2 = (bf16[1024,256]{1,0:T(8,128)(2,1)S(1)}, bf16[1024,256]{1,0:T(8,128)(2,1)}, u32[]{:S(2)}) copy-start(bf16[1024,256]{1,0:T(8,128)(2,1)} %k_ref.1) | copy-start | bytes 1572868
  0.7 24.7 %copy-start = (bf16[2048,256]{1,0:T(8,128)(2,1)S(1)}, bf16[2048,256]{1,0:T(8,128)(2,1)}, u32[]{:S(2)}) copy-start(bf16[2048,256]{1,0:T(8,128)(2,1)} %q_ref.1) | copy-start | bytes 3145732

commit v4 on v3

--- a/solution.py
+++ b/solution.py
@@ -15,6 +15,9 @@
 Y = 4
 GROUP = 4
 LATE = 16
+UNROLL = 16
+QUEUE = MOST + 1
+LENGTH = MOST + 2
 LATE_AFTER = 5
 MASKED = -1e30
 SCALE = HD ** -0.5
@@ -22,7 +25,7 @@
 MESH = pl.DeviceIdType.MESH
 F32 = jnp.float32
 BF16 = jnp.bfloat16
-VMEM_LIMIT = 16 * 1024 * 1024
+VMEM_LIMIT = 32 * 1024 * 1024
 
 
 def dot_nt(a, b):
@@ -37,32 +40,45 @@
     return lax.dot_general(a, b, (((0,), (0,)), ((), ())), preferred_element_type=F32)
 
 
+def span(index, size):
+    start = index * size
+    return pl.ds(start if isinstance(start, int) else pl.multiple_of(start, size), size)
+
+
 def picked(ref, table, row, head, first, slots):
-    cols = pl.ds(head * HD, HD)
-    parts = []
-    for slot in range(first, first + slots):
-        start = pl.multiple_of(table[row, slot] * BLOCK, BLOCK)
-        parts.append(ref[pl.ds(start, BLOCK), cols])
-    return jnp.concatenate(parts, axis=0)
-
-
-def slot_table(lists, counts_row, me, blocks_here):
-    tiles, sel = lists.shape
+    cols = span(head, HD)
+    return jnp.concatenate([ref[table[row, slot], :, cols] for slot in range(first, first + slots)], axis=0)
+
+
+def slot_table(lists, counts_rows, me, blocks_here):
+    heads, tiles, sel = lists.shape
+    rows = heads * tiles
     eye = lax.broadcasted_iota(jnp.int32, (tiles, tiles), 0) == lax.broadcasted_iota(jnp.int32, (tiles, tiles), 1)
-    counts = jnp.sum(jnp.where(eye, counts_row, 0), axis=1, keepdims=True)
-    local = lists - me * blocks_here
-    pos = lax.broadcasted_iota(jnp.int32, (tiles, sel), 1)
+    counts = jnp.concatenate(
+        [jnp.sum(jnp.where(eye, counts_rows[head : head + 1], 0), axis=1, keepdims=True) for head in range(heads)], axis=0
+    )
+    local = lists.reshape(rows, sel) - me * blocks_here
+    pos = lax.broadcasted_iota(jnp.int32, (rows, sel), 1)
     listed = (pos < counts) & (local >= 0) & (local < blocks_here)
     flags = jnp.where(listed, 1.0, 0.0)
     before = lax.broadcasted_iota(jnp.int32, (sel, sel), 0) < lax.broadcasted_iota(jnp.int32, (sel, sel), 1)
     rank = dot_nn(flags.astype(BF16), jnp.where(before, 1.0, 0.0).astype(BF16))
     ids = local.astype(F32)
-    lane = lax.broadcasted_iota(jnp.int32, (tiles, 128), 1)
+    lane = lax.broadcasted_iota(jnp.int32, (rows, 128), 1)
     total = jnp.sum(flags, axis=1, keepdims=True)
+    more = jnp.where(total > float(NEAR), 1.0, 0.0)
+    row = lax.broadcasted_iota(jnp.int32, (rows, 128), 0)
+    above = lax.broadcasted_iota(jnp.int32, (rows, rows), 1) < lax.broadcasted_iota(jnp.int32, (rows, rows), 0)
+    wide = jnp.broadcast_to(more, (rows, 128))
+    order = dot_nn(jnp.where(above, 1.0, 0.0).astype(BF16), wide.astype(BF16))
+    chosen = jnp.where((order == lane.astype(F32)) & (wide > 0.0), 1.0, 0.0)
+    queue = dot_tn(chosen.astype(BF16), row.astype(F32).astype(BF16))[:rows]
     table = jnp.where(lane == MOST, total, 0.0)
     for slot in range(MOST):
         value = jnp.sum(jnp.where(listed & (rank == float(slot)), ids, 0.0), axis=1, keepdims=True)
         table = jnp.where(lane == slot, value, table)
+    table = jnp.where(lane == QUEUE, queue, table)
+    table = jnp.where(lane == LENGTH, jnp.sum(wide, axis=0, keepdims=True), table)
     return table.astype(jnp.int32)
 
 
@@ -71,91 +87,68 @@
     return jnp.concatenate([jnp.concatenate([a, zero], axis=1), jnp.concatenate([zero, b], axis=1)], axis=0)
 
 
-def stats_kernel(heads, tiles, unroll, lists_hbm, counts_hbm, q_hbm, k_hbm, v_hbm, g_hbm,
-                 stats_ref, table_out, tops_ref, weights_ref, dprobs_ref,
-                 lists_ref, counts_ref, q_ref, k_ref, v_ref, g_ref, table, sem, table_sem):
+def slot_stats(heads, tiles, table, q_ref, k_ref, v_ref, g_ref, head, tile, first, slots):
+    row = head * tiles + tile
+    live = (table[row, MOST] - first) * BLOCK
+    rows = span(tile, TILE)
+    cols = span(head, HD)
+    keys = picked(k_ref, table, row, head, first, slots)
+    vals = picked(v_ref, table, row, head, first, slots)
+    scores = dot_nt(keys, q_ref[rows, cols]) * SCALE2
+    dprobs = dot_nt(vals, g_ref[rows, cols])
+    mask = lax.broadcasted_iota(jnp.int32, scores.shape, 0) < live
+    scores = jnp.where(mask, scores, MASKED)
+    top = jnp.max(scores, axis=0, keepdims=True)
+    weights = jnp.where(mask, jnp.exp2(scores - top), 0.0)
+    total = jnp.sum(weights, axis=0, keepdims=True)
+    delta = jnp.sum(weights * dprobs, axis=0, keepdims=True)
+    return weights, dprobs, top, total, delta
+
+
+def fetch_kernel(heads, tiles, lists_hbm, counts_hbm, q_hbm, k_hbm, v_hbm, g_hbm,
+                 stats_ref, table_out, far_tops_ref, far_weights_ref, far_dprobs_ref, q_ref, k_ref, v_ref, g_ref,
+                 lists_ref, counts_ref, table, sem, table_sem):
     me = lax.axis_index("ctx")
-    blocks_here = k_ref.shape[0] // BLOCK
-    fetches = [
-        pltpu.make_async_copy(source, target, sem.at[i])
-        for i, (source, target) in enumerate(
-            ((lists_hbm, lists_ref), (counts_hbm, counts_ref), (k_hbm, k_ref), (q_hbm, q_ref), (v_hbm, v_ref), (g_hbm, g_ref))
-        )
+    blocks_here = k_ref.shape[0]
+    pieces = [
+        (lists_hbm, lists_ref), (counts_hbm, counts_ref),
+        (k_hbm, k_ref), (v_hbm, v_ref), (q_hbm, q_ref), (g_hbm, g_ref),
     ]
+    fetches = [pltpu.make_async_copy(source, target, sem.at[i]) for i, (source, target) in enumerate(pieces)]
     for fetch in fetches:
         fetch.start()
+    stats_ref[:, 0] = jnp.full_like(stats_ref[:, 0], MASKED)
+    stats_ref[:, 1] = jnp.zeros_like(stats_ref[:, 1])
+    stats_ref[:, 2] = jnp.zeros_like(stats_ref[:, 2])
     fetches[0].wait()
     fetches[1].wait()
-    for head in range(heads):
-        table_out[pl.ds(head * tiles, tiles), :] = slot_table(
-            lists_ref[head], counts_ref[pl.ds(head, 1), :], me, blocks_here
-        )
+    table_out[...] = slot_table(lists_ref[...], counts_ref[...], me, blocks_here)
     copy = pltpu.make_async_copy(table_out, table, table_sem)
     copy.start()
     copy.wait()
     for fetch in fetches[2:]:
         fetch.wait()
 
-    def part(head, tile, first, slots):
-        row = head * tiles + tile
-        live = (table[row, MOST] - first) * BLOCK
-        rows = pl.ds(pl.multiple_of(tile * TILE, TILE), TILE)
-        cols = pl.ds(head * HD, HD)
-        keys = picked(k_ref, table, row, head, first, slots)
-        vals = picked(v_ref, table, row, head, first, slots)
-        scores = dot_nt(keys, q_ref[rows, cols]) * SCALE2
-        dprobs = dot_nt(vals, g_ref[rows, cols])
-        mask = lax.broadcasted_iota(jnp.int32, scores.shape, 0) < live
-        scores = jnp.where(mask, scores, MASKED)
-        top = jnp.max(scores, axis=0, keepdims=True)
-        weights = jnp.where(mask, jnp.exp2(scores - top), 0.0)
-        total = jnp.sum(weights, axis=0, keepdims=True)
-        delta = jnp.sum(weights * dprobs, axis=0, keepdims=True)
-        return weights, dprobs, top, total, delta
-
-    def near(step, carry):
-        for inner in range(unroll):
-            for head in range(heads):
-                tile = step * unroll + inner
-                row = head * tiles + tile
-                group = head * (tiles // GROUP) + step * (unroll // GROUP) + inner // GROUP
-                place = pl.ds(inner % GROUP, 1)
-                weights, dprobs, top, total, delta = part(head, tile, 0, NEAR)
-                weights_ref[row] = weights
-                dprobs_ref[row] = dprobs
-                tops_ref[group, place, :] = top
-                stats_ref[group, 0, place, :] = top
-                stats_ref[group, 1, place, :] = total
-                stats_ref[group, 2, place, :] = delta
+    def far(item, carry):
+        row = table[item, QUEUE]
+        group = row // GROUP
+        place = pl.ds(lax.rem(row, GROUP), 1)
+        weights, dprobs, top, total, delta = slot_stats(
+            heads, tiles, table, q_ref, k_ref, v_ref, g_ref, row // tiles, lax.rem(row, tiles), NEAR, MOST - NEAR
+        )
+        far_weights_ref[item] = weights
+        far_dprobs_ref[item] = dprobs
+        far_tops_ref[item] = top
+        stats_ref[group, 0, place, :] = top
+        stats_ref[group, 1, place, :] = total
+        stats_ref[group, 2, place, :] = delta
         return carry
 
-    lax.fori_loop(0, tiles // unroll, near, 0)
-
-    def far(step, carry):
-        for inner in range(GROUP):
-            for head in range(heads):
-                tile = step * GROUP + inner
-                row = head * tiles + tile
-                group = head * (tiles // GROUP) + step
-                place = pl.ds(inner, 1)
-
-                @pl.when(table[row, MOST] > NEAR)
-                def _():
-                    _, _, top, total, delta = part(head, tile, NEAR, MOST - NEAR)
-                    old = stats_ref[group, 0, place, :]
-                    joint = jnp.maximum(old, top)
-                    a = jnp.exp2(old - joint)
-                    b = jnp.exp2(top - joint)
-                    stats_ref[group, 0, place, :] = joint
-                    stats_ref[group, 1, place, :] = a * stats_ref[group, 1, place, :] + b * total
-                    stats_ref[group, 2, place, :] = a * stats_ref[group, 2, place, :] + b * delta
-
-        return carry
-
-    lax.fori_loop(0, tiles // GROUP, far, 0)
-
-
-def join_kernel(n_ctx, stats_ref, out_ref, zbuf, ybuf, part, merged, send1, recv1, send2, recv2, send3, recv3):
+    lax.fori_loop(0, table[0, LENGTH], far, 0)
+
+
+def join_kernel(n_ctx, heads, tiles, unroll, table, far_ref, q_ref, k_ref, v_ref, g_ref,
+                out_ref, tops_ref, weights_ref, dprobs_ref, stats_ref, zbuf, ybuf, part, merged, send1, recv1, send2, recv2, send3, recv3):
     me = lax.axis_index("ctx")
     head = lax.axis_index("head")
     n_z = n_ctx // Y
@@ -167,6 +160,32 @@
         pl.semaphore_signal(barrier, inc=1, device_id=(lax.rem(z + i, n_z) * Y + y, head), device_id_type=MESH)
     for i in range(1, Y):
         pl.semaphore_signal(barrier, inc=1, device_id=(z * Y + lax.rem(y + i, Y), head), device_id_type=MESH)
+
+    def near(step, carry):
+        for inner in range(unroll):
+            for part_head in range(heads):
+                tile = step * unroll + inner
+                row = part_head * tiles + tile
+                group = part_head * (tiles // GROUP) + step * (unroll // GROUP) + inner // GROUP
+                place = pl.ds(inner % GROUP, 1)
+                weights, dprobs, top, total, delta = slot_stats(
+                    heads, tiles, table, q_ref, k_ref, v_ref, g_ref, part_head, tile, 0, NEAR
+                )
+                weights_ref[row] = weights
+                dprobs_ref[row] = dprobs
+                tops_ref[group, place, :] = top
+                stats_ref[group, 1, place, :] = total
+                stats_ref[group, 2, place, :] = delta
+        return carry
+
+    lax.fori_loop(0, tiles // unroll, near, 0)
+    tops = tops_ref[...]
+    joint = jnp.maximum(tops, far_ref[:, 0])
+    here = jnp.exp2(tops - joint)
+    there = jnp.exp2(far_ref[:, 0] - joint)
+    stats_ref[:, 0] = joint
+    for kind in (1, 2):
+        stats_ref[:, kind] = here * stats_ref[:, kind] + there * far_ref[:, kind]
     pl.semaphore_wait(barrier, n_z + Y - 2)
 
     def first(i, source):
@@ -224,14 +243,14 @@
         third(i, z).wait_send()
 
 
-def grads_kernel(heads, tiles, unroll, table, totals_ref, tops_ref, weights_ref, dprobs_ref, q_ref, k_ref, v_ref, g_ref,
-                 dq_ref, acc):
+def grads_kernel(heads, tiles, unroll, table, totals_ref, tops_ref, weights_ref, dprobs_ref,
+                 far_tops_ref, far_weights_ref, far_dprobs_ref, q_ref, k_ref, g_ref, dq_ref, acc):
     acc[...] = jnp.zeros_like(acc)
 
     def spread(head, tile, group, place, first, probs, dprobs, keys):
         row = head * tiles + tile
-        rows = pl.ds(pl.multiple_of(tile * TILE, TILE), TILE)
-        cols = pl.ds(head * HD, HD)
+        rows = span(tile, TILE)
+        cols = span(head, HD)
         dscores = (probs * (dprobs - totals_ref[group, 1, place, :])).astype(BF16)
         both = jnp.concatenate([dscores, probs.astype(BF16)], axis=1)
         moved = dot_nn(both, diagonal(q_ref[rows, cols], g_ref[rows, cols]))
@@ -240,10 +259,10 @@
             acc[head, pl.ds(start, BLOCK), :] += moved[slot * BLOCK : (slot + 1) * BLOCK]
         return dscores
 
-    def near(step, carry):
+    for step in range(tiles // unroll):
         for inner in range(unroll):
             tile = step * unroll + inner
-            rows = pl.ds(pl.multiple_of(tile * TILE, TILE), TILE)
+            rows = span(tile, TILE)
             place = pl.ds(inner % GROUP, 1)
             pieces = []
             for head in range(heads):
@@ -257,36 +276,23 @@
                 jnp.concatenate([pieces[0][0], pieces[1][0]], axis=0), diagonal(pieces[0][1], pieces[1][1])
             )
             dq_ref[rows, :] = (moved * SCALE).astype(BF16)
+
+    def far(item, carry):
+        row = table[item, QUEUE]
+        head = row // tiles
+        tile = lax.rem(row, tiles)
+        group = row // GROUP
+        place = pl.ds(lax.rem(row, GROUP), 1)
+        rows = span(tile, TILE)
+        cols = span(head, HD)
+        share = jnp.exp2(far_tops_ref[item] - totals_ref[group, 0, place, :])
+        keys = picked(k_ref, table, row, head, NEAR, MOST - NEAR)
+        dscores = spread(head, tile, group, place, NEAR, far_weights_ref[item] * share, far_dprobs_ref[item], keys)
+        extra = dot_tn(dscores, keys) * SCALE
+        dq_ref[rows, cols] = (dq_ref[rows, cols].astype(F32) + extra).astype(BF16)
         return carry
 
-    lax.fori_loop(0, tiles // unroll, near, 0)
-
-    def far(step, carry):
-        for inner in range(GROUP):
-            for head in range(heads):
-                tile = step * GROUP + inner
-                row = head * tiles + tile
-                group = head * (tiles // GROUP) + step
-                place = pl.ds(inner, 1)
-
-                @pl.when(table[row, MOST] > NEAR)
-                def _():
-                    rows = pl.ds(pl.multiple_of(tile * TILE, TILE), TILE)
-                    cols = pl.ds(head * HD, HD)
-                    live = (table[row, MOST] - NEAR) * BLOCK
-                    keys = picked(k_ref, table, row, head, NEAR, MOST - NEAR)
-                    vals = picked(v_ref, table, row, head, NEAR, MOST - NEAR)
-                    scores = dot_nt(keys, q_ref[rows, cols]) * SCALE2
-                    dprobs = dot_nt(vals, g_ref[rows, cols])
-                    mask = lax.broadcasted_iota(jnp.int32, scores.shape, 0) < live
-                    probs = jnp.where(mask, jnp.exp2(scores - totals_ref[group, 0, place, :]), 0.0)
-                    dscores = spread(head, tile, group, place, NEAR, probs, dprobs, keys)
-                    extra = dot_tn(dscores, keys) * SCALE
-                    dq_ref[rows, cols] = (dq_ref[rows, cols].astype(F32) + extra).astype(BF16)
-
-        return carry
-
-    lax.fori_loop(0, tiles // GROUP, far, 0)
+    lax.fori_loop(0, table[0, LENGTH], far, 0)
 
 
 def leave_kernel(count, *refs):
@@ -457,38 +463,49 @@
     vmem = pl.BlockSpec(memory_space=pltpu.VMEM)
     smem = pl.BlockSpec(memory_space=pltpu.SMEM)
     hbm = pl.BlockSpec(memory_space=pltpu.HBM)
-    stats, table, tops, weights, dprobs = pl.pallas_call(
-        functools.partial(stats_kernel, heads, tiles, 4),
-        name="local_stats",
+    prefix_keys = prefix_keys.reshape(tokens // BLOCK, BLOCK, width)
+    prefix_values = prefix_values.reshape(tokens // BLOCK, BLOCK, width)
+    operands = (block_lists, list_counts, queries, prefix_keys, prefix_values, out_grad)
+    far_shape = (rows, (MOST - NEAR) * BLOCK, TILE)
+    near_shape = (rows, NEAR * BLOCK, TILE)
+    far_stats, table, *far_kept, queries, prefix_keys, prefix_values, out_grad = pl.pallas_call(
+        functools.partial(fetch_kernel, heads, tiles),
+        name="fetch",
         out_shape=(
             jax.ShapeDtypeStruct((n_z, 3, GROUP, TILE), F32),
             jax.ShapeDtypeStruct((rows, 128), jnp.int32),
-            jax.ShapeDtypeStruct((n_z, GROUP, TILE), F32),
-            jax.ShapeDtypeStruct((rows, NEAR * BLOCK, TILE), F32),
-            jax.ShapeDtypeStruct((rows, NEAR * BLOCK, TILE), F32),
+            jax.ShapeDtypeStruct((rows, 1, TILE), F32),
+            jax.ShapeDtypeStruct(far_shape, F32),
+            jax.ShapeDtypeStruct(far_shape, F32),
+            jax.ShapeDtypeStruct(queries.shape, BF16),
+            jax.ShapeDtypeStruct(prefix_keys.shape, BF16),
+            jax.ShapeDtypeStruct(prefix_values.shape, BF16),
+            jax.ShapeDtypeStruct(out_grad.shape, BF16),
         ),
         in_specs=[hbm] * 6,
-        out_specs=(vmem,) * 5,
+        out_specs=(vmem,) * 9,
         scratch_shapes=[
             pltpu.VMEM(block_lists.shape, jnp.int32),
             pltpu.VMEM(list_counts.shape, jnp.int32),
-            pltpu.VMEM(queries.shape, BF16),
-            pltpu.VMEM(prefix_keys.shape, BF16),
-            pltpu.VMEM(prefix_values.shape, BF16),
-            pltpu.VMEM(out_grad.shape, BF16),
             pltpu.SMEM((rows, 128), jnp.int32),
             pltpu.SemaphoreType.DMA((6,)),
             pltpu.SemaphoreType.DMA,
         ],
         compiler_params=pltpu.CompilerParams(vmem_limit_bytes=VMEM_LIMIT),
-    )(*[pltpu.with_memory_space_constraint(x, pltpu.HBM) for x in (block_lists, list_counts, queries, prefix_keys, prefix_values, out_grad)])
-    totals = pl.pallas_call(
-        functools.partial(join_kernel, n_ctx),
+    )(*[pltpu.with_memory_space_constraint(x, pltpu.HBM) for x in operands])
+    totals, *near_kept = pl.pallas_call(
+        functools.partial(join_kernel, n_ctx, heads, tiles, 8),
         name="join_stats",
-        out_shape=jax.ShapeDtypeStruct((n_z, 2, GROUP, TILE), F32),
-        in_specs=[vmem],
-        out_specs=vmem,
+        out_shape=(
+            jax.ShapeDtypeStruct((n_z, 2, GROUP, TILE), F32),
+            jax.ShapeDtypeStruct((n_z, GROUP, TILE), F32),
+            jax.ShapeDtypeStruct(near_shape, F32),
+            jax.ShapeDtypeStruct(near_shape, F32),
+        ),
+        in_specs=[smem] + [vmem] * 5,
+        out_specs=(vmem,) * 4,
         scratch_shapes=[
+            pltpu.VMEM((n_z, 3, GROUP, TILE), F32),
             pltpu.VMEM((n_z, 3, GROUP, TILE), F32),
             pltpu.VMEM((Y, 3, GROUP, TILE), F32),
             pltpu.VMEM((3, GROUP, TILE), F32),
@@ -500,8 +517,8 @@
             pltpu.SemaphoreType.DMA((n_z,)),
             pltpu.SemaphoreType.DMA((n_z,)),
         ],
-        compiler_params=pltpu.CompilerParams(collective_id=0, has_side_effects=True, vmem_limit_bytes=VMEM_LIMIT),
-    )(stats)
+        compiler_params=pltpu.CompilerParams(collective_id=0, has_side_effects=True, vmem_limit_bytes=VMEM_LIMIT // 2),
+    )(table, far_stats, queries, prefix_keys, prefix_values, out_grad)
     dq, acc = pl.pallas_call(
         functools.partial(grads_kernel, heads, tiles, 4),
         name="local_grads",
@@ -509,10 +526,10 @@
             jax.ShapeDtypeStruct((latents, width), BF16),
             jax.ShapeDtypeStruct((heads, tokens, 2 * HD), F32),
         ),
-        in_specs=[smem] + [vmem] * 8,
+        in_specs=[smem] + [vmem] * 10,
         out_specs=(vmem, vmem),
         compiler_params=pltpu.CompilerParams(vmem_limit_bytes=VMEM_LIMIT),
-    )(table, totals, tops, weights, dprobs, queries, prefix_keys, prefix_values, out_grad)
+    )(table, totals, *near_kept, *far_kept, queries, prefix_keys, out_grad)
     piece = tokens // n_head
     results = pl.pallas_call(
         functools.partial(swap_kernel, n_ctx, n_head),
@@ -545,7 +562,7 @@
             pltpu.SemaphoreType.DMA((Y,)),
             pltpu.SemaphoreType.DMA((2,)),
         ],
-        compiler_params=pltpu.CompilerParams(collective_id=1, has_side_effects=True, vmem_limit_bytes=VMEM_LIMIT),
+        compiler_params=pltpu.CompilerParams(collective_id=1, has_side_effects=True, vmem_limit_bytes=VMEM_LIMIT // 2),
     )(dq.reshape(n_z, Y, own, width), acc)
     return pl.pallas_call(
         functools.partial(leave_kernel, len(results)),

time: 50.3 us -> 48 us (0.954)
  Pallas kernels: 49.5 us -> 47.2 us
    pallas_call x2, Pallas kernels: 24.6 us -> 22.8 us  [the longest x1 20.6 us: local(): pl.pallas_call(functools.partial(join_kernel, n_ctx, heads, tiles, 8), na...]
    pallas_call x1, Pallas kernels: 3.66 us -> 2.08 us  [local(): pl.pallas_call(functools.partial(grads_kernel, heads, tiles, 4), name='lo...]
    pallas_call x1, Pallas kernels: 20.3 us -> 21.4 us  [local(): pl.pallas_call(functools.partial(swap_kernel, n_ctx, n_head), name='swap_...]
where the time goes in v4:
time: 48 us; the launch traced here: 47.9 us
  Pallas kernels  47.2 us (98%)
  between operations  0.66 us (1%)
    pallas_call x1, Pallas kernels, local(): pl.pallas_call(functools.partial(swap_kernel, n_ctx, n_head), name='swap_...  21.4 us
    pallas_call x1, Pallas kernels, local(): pl.pallas_call(functools.partial(join_kernel, n_ctx, heads, tiles, 8), na...  20.6 us
    pallas_call x1, Pallas kernels, local(): pl.pallas_call(functools.partial(fetch_kernel, heads, tiles), name='fetch...  2.14 us
    pallas_call x1, Pallas kernels, local(): pl.pallas_call(functools.partial(grads_kernel, heads, tiles, 4), name='lo...  2.08 us
    pallas_call x1, Pallas kernels, local(): pl.pallas_call(functools.partial(leave_kernel, len(results)), name='leave...  1.01 us

profile of v4, /device:TPU:1, one launch (start us, length us, event | category | flops | bytes accessed | tf_op | source)
XLA Modules:
  0.0 47.9 jit_solution(2653719454405953642)
XLA Ops:
  0.6 2.1 %fetch.1 = (f32[8,3,4,128]{3,2,1,0:T(4,128)S(1)}, s32[32,128]{1,0:T(8,128)S(1)}, f32[32,1,128]{2,1,0:T(1,128)S(1)}, f32[32,384,128]{2,1,0:T(8,128)S(1)}, f32[32,...) custom-call(s32[2,16,64]{2,1,0:T(8,128)} %lists_hbm.1, ...), custom_call_target="tpu_custom_call" | custom-call | tf_op jit(solution)/shard_map/fetch/pallas_call | solution.py:471
  2.8 20.6 %join_stats.1 = (f32[8,2,4,128]{3,2,1,0:T(4,128)S(1)}, f32[8,4,128]{2,1,0:T(4,128)S(1)}, f32[32,128,128]{2,1,0:T(8,128)S(1)}, f32[32,128,128]{2,1,0:T(8,128)S(1)}) custom-call(s32[32,128]{1,0:T(8,128)S(1)} %get-tuple-element.21.table, f32[8,3,4,128]{3,2,1,0:T(4,128)S(1)} %get-tuple-element.22.far_ref, bf16[2048,256]{1,0:T(8,128)(2,1)S(1)} %get-tuple-element.23.q_ref, ...), custom_call_target="tpu_custom_call" | custom-call | tf_op jit(solution)/shard_map/join_stats/pallas_call | solution.py:496
  23.4 2.1 %local_grads.1 = (bf16[2048,256]{1,0:T(8,128)(2,1)S(1)}, f32[2,1024,256]{2,1,0:T(8,128)S(1)}) custom-call(s32[32,128]{1,0:T(8,128)S(1)} %get-tuple-element.21.table, f32[8,2,4,128]{3,2,1,0:T(4,128)S(1)} %get-tuple-element.27.totals_ref, f32[8,4,128]{2,1,0:T(4,128)S(1)} %get-tuple-element.28.tops_ref, f32[32,128,128]{2,1,0:T(8,128)S(1)} %get-tuple-element.29.weights_ref, ...), custom_call_target="tpu_custom_call" | custom-call | tf_op jit(solution)/shard_map/local_grads/pallas_call | solution.py:522
  25.5 21.4 %swap_grads.1 = (bf16[64,256]{1,0:T(8,128)(2,1)S(1)}, bf16[128,2048]{1,0:T(8,128)(2,1)S(1)}, bf16[128,2048]{1,0:T(8,128)(2,1)S(1)}) custom-call(bf16[8,4,64,256]{3,2,1,0:T(8,128)(2,1)S(1)} %bitcast.3, f32[2,1024,256]{2,1,0:T(8,128)S(1)} %get-tuple-element.35.acc_ref), custom_call_target="tpu_custom_call" | custom-call | tf_op jit(solution)/shard_map/swap_grads/pallas_call | solution.py:534
  46.9 1.0 %leave.1 = (bf16[64,256]{1,0:T(8,128)(2,1)}, bf16[128,2048]{1,0:T(8,128)(2,1)}, bf16[128,2048]{1,0:T(8,128)(2,1)}) custom-call(bf16[64,256]{1,0:T(8,128)(2,1)S(1)} %get-tuple-element.36.refs_0_, bf16[128,2048]{1,0:T(8,128)(2,1)S(1)} %get-tuple-element.37.refs_1_, bf16[128,2048]{1,0:T(8,128)(2,1)S(1)} %get-tuple-element.38.refs_2_), custom_call_target="tpu_custom_call" | custom-call | tf_op jit(solution)/shard_map/leave/pallas_call | solution.py:567

commit v5 on v4

--- a/solution.py
+++ b/solution.py
@@ -14,6 +14,7 @@
 NEAR = 2
 Y = 4
 GROUP = 4
+PAIR = 2
 LATE = 16
 UNROLL = 16
 QUEUE = MOST + 1
@@ -87,6 +88,11 @@
     return jnp.concatenate([jnp.concatenate([a, zero], axis=1), jnp.concatenate([zero, b], axis=1)], axis=0)
 
 
+def seat(head, tile):
+    inner = tile % PAIR if isinstance(tile, int) else lax.rem(tile, PAIR)
+    return tile // PAIR, pl.ds(head * PAIR + inner, 1)
+
+
 def slot_stats(heads, tiles, table, q_ref, k_ref, v_ref, g_ref, head, tile, first, slots):
     row = head * tiles + tile
     live = (table[row, MOST] - first) * BLOCK
@@ -131,10 +137,11 @@
 
     def far(item, carry):
         row = table[item, QUEUE]
-        group = row // GROUP
-        place = pl.ds(lax.rem(row, GROUP), 1)
+        head = row // tiles
+        tile = lax.rem(row, tiles)
+        group, place = seat(head, tile)
         weights, dprobs, top, total, delta = slot_stats(
-            heads, tiles, table, q_ref, k_ref, v_ref, g_ref, row // tiles, lax.rem(row, tiles), NEAR, MOST - NEAR
+            heads, tiles, table, q_ref, k_ref, v_ref, g_ref, head, tile, NEAR, MOST - NEAR
         )
         far_weights_ref[item] = weights
         far_dprobs_ref[item] = dprobs
@@ -147,8 +154,8 @@
     lax.fori_loop(0, table[0, LENGTH], far, 0)
 
 
-def join_kernel(n_ctx, heads, tiles, unroll, table, far_ref, q_ref, k_ref, v_ref, g_ref,
-                out_ref, tops_ref, weights_ref, dprobs_ref, stats_ref, zbuf, ybuf, part, merged, send1, recv1, send2, recv2, send3, recv3):
+def join_kernel(n_ctx, heads, tiles, segments, table, far_ref, q_ref, k_ref, v_ref, g_ref,
+                out_ref, acc_ref, tops_ref, weights_ref, dprobs_ref, stats_ref, zbuf, ybuf, part, merged, send1, recv1, send2, recv2, send3, recv3):
     me = lax.axis_index("ctx")
     head = lax.axis_index("head")
     n_z = n_ctx // Y
@@ -161,13 +168,13 @@
     for i in range(1, Y):
         pl.semaphore_signal(barrier, inc=1, device_id=(z * Y + lax.rem(y + i, Y), head), device_id_type=MESH)
 
-    def near(step, carry):
-        for inner in range(unroll):
+    def near(step):
+        group = lax.rem(z + step, n_z)
+        for inner in range(PAIR):
             for part_head in range(heads):
-                tile = step * unroll + inner
+                tile = group * PAIR + inner
                 row = part_head * tiles + tile
-                group = part_head * (tiles // GROUP) + step * (unroll // GROUP) + inner // GROUP
-                place = pl.ds(inner % GROUP, 1)
+                place = pl.ds(part_head * PAIR + inner, 1)
                 weights, dprobs, top, total, delta = slot_stats(
                     heads, tiles, table, q_ref, k_ref, v_ref, g_ref, part_head, tile, 0, NEAR
                 )
@@ -176,17 +183,18 @@
                 tops_ref[group, place, :] = top
                 stats_ref[group, 1, place, :] = total
                 stats_ref[group, 2, place, :] = delta
-        return carry
-
-    lax.fori_loop(0, tiles // unroll, near, 0)
-    tops = tops_ref[...]
-    joint = jnp.maximum(tops, far_ref[:, 0])
-    here = jnp.exp2(tops - joint)
-    there = jnp.exp2(far_ref[:, 0] - joint)
-    stats_ref[:, 0] = joint
-    for kind in (1, 2):
-        stats_ref[:, kind] = here * stats_ref[:, kind] + there * far_ref[:, kind]
-    pl.semaphore_wait(barrier, n_z + Y - 2)
+
+    def merge(step):
+        group = lax.rem(z + step, n_z)
+        tops = tops_ref[group]
+        others = far_ref[group, 0]
+        joint = jnp.maximum(tops, others)
+        here = jnp.exp2(tops - joint)
+        there = jnp.exp2(others - joint)
+        stats_ref[group, 0] = joint
+        for kind in (1, 2):
+            stats_ref[group, kind] = here * stats_ref[group, kind] + there * far_ref[group, kind]
+
 
     def first(i, source):
         peer = lax.rem(z + i, n_z)
@@ -215,9 +223,20 @@
         share = jnp.exp2(tops - top[None])
         return top, jnp.sum(share * pieces[:, 1], axis=0), jnp.sum(share * pieces[:, 2], axis=0)
 
-    for i in far_first:
-        first(i, z).start()
+    order = far_first + [0]
+    for begin in range(0, n_z, n_z // segments):
+        steps = order[begin : begin + n_z // segments]
+        for i in steps:
+            near(i)
+        for i in steps:
+            merge(i)
+        if begin == 0:
+            pl.semaphore_wait(barrier, n_z + Y - 2)
+        for i in steps:
+            if i > 0:
+                first(i, z).start()
     zbuf[z] = stats_ref[z]
+    acc_ref[...] = jnp.zeros_like(acc_ref)
     for i in range(1, n_z):
         first(i, lax.rem(z + i, n_z)).wait_recv()
     for kind, value in enumerate(combine(zbuf[...])):
@@ -244,8 +263,7 @@
 
 
 def grads_kernel(heads, tiles, unroll, table, totals_ref, tops_ref, weights_ref, dprobs_ref,
-                 far_tops_ref, far_weights_ref, far_dprobs_ref, q_ref, k_ref, g_ref, dq_ref, acc):
-    acc[...] = jnp.zeros_like(acc)
+                 far_tops_ref, far_weights_ref, far_dprobs_ref, q_ref, k_ref, g_ref, zeros_ref, dq_ref, acc):
 
     def spread(head, tile, group, place, first, probs, dprobs, keys):
         row = head * tiles + tile
@@ -263,11 +281,10 @@
         for inner in range(unroll):
             tile = step * unroll + inner
             rows = span(tile, TILE)
-            place = pl.ds(inner % GROUP, 1)
             pieces = []
             for head in range(heads):
                 row = head * tiles + tile
-                group = head * (tiles // GROUP) + step * (unroll // GROUP) + inner // GROUP
+                group, place = seat(head, tile)
                 share = jnp.exp2(tops_ref[group, place, :] - totals_ref[group, 0, place, :])
                 keys = picked(k_ref, table, row, head, 0, NEAR)
                 dscores = spread(head, tile, group, place, 0, weights_ref[row] * share, dprobs_ref[row], keys)
@@ -281,8 +298,7 @@
         row = table[item, QUEUE]
         head = row // tiles
         tile = lax.rem(row, tiles)
-        group = row // GROUP
-        place = pl.ds(lax.rem(row, GROUP), 1)
+        group, place = seat(head, tile)
         rows = span(tile, TILE)
         cols = span(head, HD)
         share = jnp.exp2(far_tops_ref[item] - totals_ref[group, 0, place, :])
@@ -493,17 +509,18 @@
         ],
         compiler_params=pltpu.CompilerParams(vmem_limit_bytes=VMEM_LIMIT),
     )(*[pltpu.with_memory_space_constraint(x, pltpu.HBM) for x in operands])
-    totals, *near_kept = pl.pallas_call(
-        functools.partial(join_kernel, n_ctx, heads, tiles, 8),
+    totals, zeros, *near_kept = pl.pallas_call(
+        functools.partial(join_kernel, n_ctx, heads, tiles, 4),
         name="join_stats",
         out_shape=(
             jax.ShapeDtypeStruct((n_z, 2, GROUP, TILE), F32),
+            jax.ShapeDtypeStruct((heads, tokens, 2 * HD), F32),
             jax.ShapeDtypeStruct((n_z, GROUP, TILE), F32),
             jax.ShapeDtypeStruct(near_shape, F32),
             jax.ShapeDtypeStruct(near_shape, F32),
         ),
         in_specs=[smem] + [vmem] * 5,
-        out_specs=(vmem,) * 4,
+        out_specs=(vmem,) * 5,
         scratch_shapes=[
             pltpu.VMEM((n_z, 3, GROUP, TILE), F32),
             pltpu.VMEM((n_z, 3, GROUP, TILE), F32),
@@ -526,10 +543,11 @@
             jax.ShapeDtypeStruct((latents, width), BF16),
             jax.ShapeDtypeStruct((heads, tokens, 2 * HD), F32),
         ),
-        in_specs=[smem] + [vmem] * 10,
+        in_specs=[smem] + [vmem] * 11,
         out_specs=(vmem, vmem),
+        input_output_aliases={11: 1},
         compiler_params=pltpu.CompilerParams(vmem_limit_bytes=VMEM_LIMIT),
-    )(table, totals, *near_kept, *far_kept, queries, prefix_keys, out_grad)
+    )(table, totals, *near_kept, *far_kept, queries, prefix_keys, out_grad, zeros)
     piece = tokens // n_head
     results = pl.pallas_call(
         functools.partial(swap_kernel, n_ctx, n_head),

time: 48 us -> 48 us (level)
  no operation moved by 1% of the time
where the time goes in v5:
time: 48 us; the launch traced here: 47.8 us
  Pallas kernels  47.2 us (98%)
  between operations  0.66 us (1%)
    pallas_call x1, Pallas kernels, local(): pl.pallas_call(functools.partial(swap_kernel, n_ctx, n_head), name='swap_...  21.5 us
    pallas_call x1, Pallas kernels, local(): pl.pallas_call(functools.partial(join_kernel, n_ctx, heads, tiles, 4), na...  20.6 us
    pallas_call x1, Pallas kernels, local(): pl.pallas_call(functools.partial(fetch_kernel, heads, tiles), name='fetch...  2.14 us
    pallas_call x1, Pallas kernels, local(): pl.pallas_call(functools.partial(grads_kernel, heads, tiles, 4), name='lo...  1.92 us
    pallas_call x1, Pallas kernels, local(): pl.pallas_call(functools.partial(leave_kernel, len(results)), name='leave...  1.01 us

profile of v5, /device:TPU:1, one launch (start us, length us, event | category | flops | bytes accessed | tf_op | source)
XLA Modules:
  0.0 47.8 jit_solution(15388630266287890965)
XLA Ops:
  0.6 2.1 %fetch.1 = (f32[8,3,4,128]{3,2,1,0:T(4,128)S(1)}, s32[32,128]{1,0:T(8,128)S(1)}, f32[32,1,128]{2,1,0:T(1,128)S(1)}, f32[32,384,128]{2,1,0:T(8,128)S(1)}, f32[32,...) custom-call(s32[2,16,64]{2,1,0:T(8,128)} %lists_hbm.1, ...), custom_call_target="tpu_custom_call" | custom-call | tf_op jit(solution)/shard_map/fetch/pallas_call | solution.py:487
  2.8 20.6 %join_stats.1 = (f32[8,2,4,128]{3,2,1,0:T(4,128)S(1)}, f32[2,1024,256]{2,1,0:T(8,128)S(1)}, f32[8,4,128]{2,1,0:T(4,128)S(1)}, f32[32,128,128]{2,1,0:T(8,128)S(1)}, f32[32,128,128]{2,1,0:T(8,128)S(1)}) custom-call(s32[32,128]{1,0:T(8,128)S(1)} %get-tuple-element.22.table, f32[8,3,4,128]{3,2,1,0:T(4,128)S(1)} %get-tuple-element.23.far_ref, ...), custom_call_target="tpu_custom_call" | custom-call | tf_op jit(solution)/shard_map/join_stats/pallas_call | solution.py:512
  23.4 1.9 %local_grads.1 = (bf16[2048,256]{1,0:T(8,128)(2,1)S(1)}, f32[2,1024,256]{2,1,0:T(8,128)S(1)}) custom-call(s32[32,128]{1,0:T(8,128)S(1)} %get-tuple-element.22.table, f32[8,2,4,128]{3,2,1,0:T(4,128)S(1)} %get-tuple-element.28.totals_ref, f32[8,4,128]{2,1,0:T(4,128)S(1)} %get-tuple-element.29.tops_ref, ...), custom_call_target="tpu_custom_call", output_to_operand_aliasing={{1}: (11, {})} | custom-call | tf_op jit(solution)/shard_map/local_grads/pallas_call | solution.py:539
  25.3 21.5 %swap_grads.1 = (bf16[64,256]{1,0:T(8,128)(2,1)S(1)}, bf16[128,2048]{1,0:T(8,128)(2,1)S(1)}, bf16[128,2048]{1,0:T(8,128)(2,1)S(1)}) custom-call(bf16[8,4,64,256]{3,2,1,0:T(8,128)(2,1)S(1)} %bitcast.3, f32[2,1024,256]{2,1,0:T(8,128)S(1)} %get-tuple-element.37.acc_ref), custom_call_target="tpu_custom_call" | custom-call | tf_op jit(solution)/shard_map/swap_grads/pallas_call | solution.py:552
  46.8 1.0 %leave.1 = (bf16[64,256]{1,0:T(8,128)(2,1)}, bf16[128,2048]{1,0:T(8,128)(2,1)}, bf16[128,2048]{1,0:T(8,128)(2,1)}) custom-call(bf16[64,256]{1,0:T(8,128)(2,1)S(1)} %get-tuple-element.38.refs_0_, bf16[128,2048]{1,0:T(8,128)(2,1)S(1)} %get-tuple-element.39.refs_1_, bf16[128,2048]{1,0:T(8,128)(2,1)S(1)} %get-tuple-element.40.refs_2_), custom_call_target="tpu_custom_call" | custom-call | tf_op jit(solution)/shard_map/leave/pallas_call | solution.py:585

commit v6 on v5

--- a/solution.py
+++ b/solution.py
@@ -151,7 +151,12 @@
         stats_ref[group, 2, place, :] = delta
         return carry
 
-    lax.fori_loop(0, table[0, LENGTH], far, 0)
+    def two(step, carry):
+        far(2 * step, 0)
+        far(2 * step + 1, 0)
+        return carry
+
+    lax.fori_loop(0, lax.div(table[0, LENGTH] + 1, 2), two, 0)
 
 
 def join_kernel(n_ctx, heads, tiles, segments, table, far_ref, q_ref, k_ref, v_ref, g_ref,
@@ -302,13 +307,19 @@
         rows = span(tile, TILE)
         cols = span(head, HD)
         share = jnp.exp2(far_tops_ref[item] - totals_ref[group, 0, place, :])
+        share = jnp.where(item < table[0, LENGTH], share, 0.0)
         keys = picked(k_ref, table, row, head, NEAR, MOST - NEAR)
         dscores = spread(head, tile, group, place, NEAR, far_weights_ref[item] * share, far_dprobs_ref[item], keys)
         extra = dot_tn(dscores, keys) * SCALE
         dq_ref[rows, cols] = (dq_ref[rows, cols].astype(F32) + extra).astype(BF16)
         return carry
 
-    lax.fori_loop(0, table[0, LENGTH], far, 0)
+    def two(step, carry):
+        far(2 * step, 0)
+        far(2 * step + 1, 0)
+        return carry
+
+    lax.fori_loop(0, lax.div(table[0, LENGTH] + 1, 2), two, 0)
 
 
 def leave_kernel(count, *refs):

time: 48 us -> 47.4 us (0.987)
  Pallas kernels: 47.2 us -> 46.3 us
    pallas_call x1, Pallas kernels: 21.5 us -> 20.3 us  [local(): pl.pallas_call(functools.partial(swap_kernel, n_ctx, n_head), name='swap_...]
where the time goes in v6:
time: 47.4 us; the launch traced here: 47 us
  Pallas kernels  46.3 us (98%)
  between operations  0.66 us (1%)
    pallas_call x1, Pallas kernels, local(): pl.pallas_call(functools.partial(join_kernel, n_ctx, heads, tiles, 4), na...  20.9 us
    pallas_call x1, Pallas kernels, local(): pl.pallas_call(functools.partial(swap_kernel, n_ctx, n_head), name='swap_...  20.3 us
    pallas_call x1, Pallas kernels, local(): pl.pallas_call(functools.partial(fetch_kernel, heads, tiles), name='fetch...  2.14 us
    pallas_call x1, Pallas kernels, local(): pl.pallas_call(functools.partial(grads_kernel, heads, tiles, 4), name='lo...  1.93 us
    pallas_call x1, Pallas kernels, local(): pl.pallas_call(functools.partial(leave_kernel, len(results)), name='leave...  1.01 us

profile of v6, /device:TPU:1, one launch (start us, length us, event | category | flops | bytes accessed | tf_op | source)
XLA Modules:
  0.0 47.0 jit_solution(8109027929122228100)
XLA Ops:
  0.6 2.1 %fetch.1 = (f32[8,3,4,128]{3,2,1,0:T(4,128)S(1)}, s32[32,128]{1,0:T(8,128)S(1)}, f32[32,1,128]{2,1,0:T(1,128)S(1)}, f32[32,384,128]{2,1,0:T(8,128)S(1)}, f32[32,...) custom-call(s32[2,16,64]{2,1,0:T(8,128)} %lists_hbm.1, ...), custom_call_target="tpu_custom_call" | custom-call | tf_op jit(solution)/shard_map/fetch/pallas_call | solution.py:498
  2.8 20.9 %join_stats.1 = (f32[8,2,4,128]{3,2,1,0:T(4,128)S(1)}, f32[2,1024,256]{2,1,0:T(8,128)S(1)}, f32[8,4,128]{2,1,0:T(4,128)S(1)}, f32[32,128,128]{2,1,0:T(8,128)S(1)}, f32[32,128,128]{2,1,0:T(8,128)S(1)}) custom-call(s32[32,128]{1,0:T(8,128)S(1)} %get-tuple-element.22.table, f32[8,3,4,128]{3,2,1,0:T(4,128)S(1)} %get-tuple-element.23.far_ref, ...), custom_call_target="tpu_custom_call" | custom-call | tf_op jit(solution)/shard_map/join_stats/pallas_call | solution.py:523
  23.7 1.9 %local_grads.1 = (bf16[2048,256]{1,0:T(8,128)(2,1)S(1)}, f32[2,1024,256]{2,1,0:T(8,128)S(1)}) custom-call(s32[32,128]{1,0:T(8,128)S(1)} %get-tuple-element.22.table, f32[8,2,4,128]{3,2,1,0:T(4,128)S(1)} %get-tuple-element.28.totals_ref, f32[8,4,128]{2,1,0:T(4,128)S(1)} %get-tuple-element.29.tops_ref, ...), custom_call_target="tpu_custom_call", output_to_operand_aliasing={{1}: (11, {})} | custom-call | tf_op jit(solution)/shard_map/local_grads/pallas_call | solution.py:550
  25.6 20.3 %swap_grads.1 = (bf16[64,256]{1,0:T(8,128)(2,1)S(1)}, bf16[128,2048]{1,0:T(8,128)(2,1)S(1)}, bf16[128,2048]{1,0:T(8,128)(2,1)S(1)}) custom-call(bf16[8,4,64,256]{3,2,1,0:T(8,128)(2,1)S(1)} %bitcast.3, f32[2,1024,256]{2,1,0:T(8,128)S(1)} %get-tuple-element.37.acc_ref), custom_call_target="tpu_custom_call" | custom-call | tf_op jit(solution)/shard_map/swap_grads/pallas_call | solution.py:563
  46.0 1.0 %leave.1 = (bf16[64,256]{1,0:T(8,128)(2,1)}, bf16[128,2048]{1,0:T(8,128)(2,1)}, bf16[128,2048]{1,0:T(8,128)(2,1)}) custom-call(bf16[64,256]{1,0:T(8,128)(2,1)S(1)} %get-tuple-element.38.refs_0_, bf16[128,2048]{1,0:T(8,128)(2,1)S(1)} %get-tuple-element.39.refs_1_, bf16[128,2048]{1,0:T(8,128)(2,1)S(1)} %get-tuple-element.40.refs_2_), custom_call_target="tpu_custom_call" | custom-call | tf_op jit(solution)/shard_map/leave/pallas_call | solution.py:596

commit v7 on v6

--- a/solution.py
+++ b/solution.py
@@ -15,6 +15,7 @@
 Y = 4
 GROUP = 4
 PAIR = 2
+PARTS = 4
 LATE = 16
 UNROLL = 16
 QUEUE = MOST + 1
@@ -324,7 +325,12 @@
 
 def leave_kernel(count, *refs):
     sem = refs[2 * count]
-    copies = [pltpu.make_async_copy(refs[i], refs[count + i], sem.at[i]) for i in range(count)]
+    copies = []
+    for i in range(count):
+        part = refs[i].shape[0] // PARTS
+        for j in range(PARTS):
+            rows = pl.ds(j * part, part)
+            copies.append(pltpu.make_async_copy(refs[i].at[rows], refs[count + i].at[rows], sem.at[i, j]))
     for copy in copies:
         copy.start()
     for copy in copies:
@@ -599,7 +605,7 @@
         out_shape=tuple(jax.ShapeDtypeStruct(result.shape, result.dtype) for result in results),
         in_specs=[vmem] * len(results),
         out_specs=(hbm,) * len(results),
-        scratch_shapes=[pltpu.SemaphoreType.DMA((len(results),))],
+        scratch_shapes=[pltpu.SemaphoreType.DMA((len(results), PARTS))],
         compiler_params=pltpu.CompilerParams(vmem_limit_bytes=VMEM_LIMIT),
     )(*results)
 

time: 47.4 us -> 47.4 us (level)
  no operation moved by 1% of the time
where the time goes in v7:
time: 47.4 us; the launch traced here: 47.2 us
  Pallas kernels  46.5 us (98%)
  between operations  0.66 us (1%)
    pallas_call x1, Pallas kernels, local(): pl.pallas_call(functools.partial(join_kernel, n_ctx, heads, tiles, 4), na...  20.8 us
    pallas_call x1, Pallas kernels, local(): pl.pallas_call(functools.partial(swap_kernel, n_ctx, n_head), name='swap_...  19.9 us
    pallas_call x1, Pallas kernels, local(): pl.pallas_call(functools.partial(fetch_kernel, heads, tiles), name='fetch...  2.54 us
    pallas_call x1, Pallas kernels, local(): pl.pallas_call(functools.partial(grads_kernel, heads, tiles, 4), name='lo...  2.3 us
    pallas_call x1, Pallas kernels, local(): pl.pallas_call(functools.partial(leave_kernel, len(results)), name='leave...  1.08 us

profile of v7, /device:TPU:1, one launch (start us, length us, event | category | flops | bytes accessed | tf_op | source)
XLA Modules:
  0.0 47.2 jit_solution(5048334105558479119)
XLA Ops:
  0.6 2.5 %fetch.1 = (f32[8,3,4,128]{3,2,1,0:T(4,128)S(1)}, s32[32,128]{1,0:T(8,128)S(1)}, f32[32,1,128]{2,1,0:T(1,128)S(1)}, f32[32,384,128]{2,1,0:T(8,128)S(1)}, f32[32,...) custom-call(s32[2,16,64]{2,1,0:T(8,128)} %lists_hbm.1, ...), custom_call_target="tpu_custom_call" | custom-call | tf_op jit(solution)/shard_map/fetch/pallas_call | solution.py:504
  3.2 20.8 %join_stats.1 = (f32[8,2,4,128]{3,2,1,0:T(4,128)S(1)}, f32[2,1024,256]{2,1,0:T(8,128)S(1)}, f32[8,4,128]{2,1,0:T(4,128)S(1)}, f32[32,128,128]{2,1,0:T(8,128)S(1)}, f32[32,128,128]{2,1,0:T(8,128)S(1)}) custom-call(s32[32,128]{1,0:T(8,128)S(1)} %get-tuple-element.22.table, f32[8,3,4,128]{3,2,1,0:T(4,128)S(1)} %get-tuple-element.23.far_ref, ...), custom_call_target="tpu_custom_call" | custom-call | tf_op jit(solution)/shard_map/join_stats/pallas_call | solution.py:529
  23.9 2.3 %local_grads.1 = (bf16[2048,256]{1,0:T(8,128)(2,1)S(1)}, f32[2,1024,256]{2,1,0:T(8,128)S(1)}) custom-call(s32[32,128]{1,0:T(8,128)S(1)} %get-tuple-element.22.table, f32[8,2,4,128]{3,2,1,0:T(4,128)S(1)} %get-tuple-element.28.totals_ref, f32[8,4,128]{2,1,0:T(4,128)S(1)} %get-tuple-element.29.tops_ref, ...), custom_call_target="tpu_custom_call", output_to_operand_aliasing={{1}: (11, {})} | custom-call | tf_op jit(solution)/shard_map/local_grads/pallas_call | solution.py:556
  26.2 19.9 %swap_grads.1 = (bf16[64,256]{1,0:T(8,128)(2,1)S(1)}, bf16[128,2048]{1,0:T(8,128)(2,1)S(1)}, bf16[128,2048]{1,0:T(8,128)(2,1)S(1)}) custom-call(bf16[8,4,64,256]{3,2,1,0:T(8,128)(2,1)S(1)} %bitcast.3, f32[2,1024,256]{2,1,0:T(8,128)S(1)} %get-tuple-element.37.acc_ref), custom_call_target="tpu_custom_call" | custom-call | tf_op jit(solution)/shard_map/swap_grads/pallas_call | solution.py:569
  46.1 1.1 %leave.1 = (bf16[64,256]{1,0:T(8,128)(2,1)}, bf16[128,2048]{1,0:T(8,128)(2,1)}, bf16[128,2048]{1,0:T(8,128)(2,1)}) custom-call(bf16[64,256]{1,0:T(8,128)(2,1)S(1)} %get-tuple-element.38.refs_0_, bf16[128,2048]{1,0:T(8,128)(2,1)S(1)} %get-tuple-element.39.refs_1_, bf16[128,2048]{1,0:T(8,128)(2,1)S(1)} %get-tuple-element.40.refs_2_), custom_call_target="tpu_custom_call" | custom-call | tf_op jit(solution)/shard_map/leave/pallas_call | solution.py:602
